TPU v7x, 32 devices: a whole 2x2x4 slice. The times are simulated.
32 devices in a mesh: chain: 8 (over z, x), pts: 4 (over y, core).
Axes of the slice: x: 2, y: 2, z: 4, core: 2. Of those that a mesh axis runs over, the one named last changes fastest.
Arguments:
- cam_jac: bfloat16 [2048, 12, 512], P(('chain', 'pts')), may hold values from -0.125 to 0.125
- point_jac: bfloat16 [2048, 6, 512], P(('chain', 'pts')), may hold values from -1.5 to 1.5
- residual: float32 [2048, 2, 512], P(('chain', 'pts')), may hold values from -6 to 6
- obs_cam: int32 [2048, 8], P(('chain', 'pts')), may hold values from 0 to 63, all different within a row; in each aligned block of 64 rows (0 to 63, 64 to 127, ...) at most 8 rows name the same one
- damp_exp: int32 [2, 64], replicated, may hold values from -3 to 0
- cam_step: float32 [64, 384], P('chain'), may hold values from -6 to 6
- diag_inverse: bfloat16 [64, 384, 384], P('chain'), may hold values from -0.06 to 0.56
- coupling: bfloat16 [64, 384, 384], P('chain'), may hold values from -33 to 9
Outputs:
- cam_out: float32 [64, 384], P('chain')
- point_out: float32 [2048, 3, 64], P(('chain', 'pts'))
Inputs may be any that keep to these rules, and one draw needn't show every extreme that they name: `obs_cam`: in the point blocks of one device no camera block is named by more than 8 of them, and some camera block is named by exactly 8; each row names 8 different camera blocks, and every camera block is named somewhere.
All inputs are finite; a program needn't handle non-finite values.
Results may differ from a plain program's by a relative error of at most 0.0003.
Values sent between devices are 32-bit elements; how exact they have to be, the bound alone decides.
A program may use at most 192 MiB of HBM per device.

v0:
```python
import jax
import jax.numpy as jnp
from jax import lax
from jax.sharding import PartitionSpec as P

ITERS = 2


exact_mode = lax.Precision.HIGHEST


def entering(x, axis, combine, identity, reverse):
    peers, here = (lax.axis_size(axis), lax.axis_index(axis))
    everything = jax.tree.map(lambda part: lax.all_gather(part, axis), x)
    start = jax.tree.map(
        lambda part, zero: jnp.broadcast_to(jnp.asarray(zero, part.dtype), part.shape), x, identity
    )

    def turn(k, before):
        at = peers - 1 - k if reverse else k
        reached = at > here if reverse else at < here
        new = combine(before, jax.tree.map(lambda part: part[at], everything))
        return jax.tree.map(lambda a, b: jnp.where(reached, a, b), new, before)

    return lax.fori_loop(0, peers, turn, start)


def solve_three(hessian, target):
    aa_entry = hessian[:, 0, 0]
    ab_entry = hessian[:, 0, 1]
    ac_entry = hessian[:, 0, 2]
    bb_entry = hessian[:, 1, 1]
    bc_entry = hessian[:, 1, 2]
    cc_entry = hessian[:, 2, 2]
    cof_aa = bb_entry * cc_entry - bc_entry * bc_entry
    cof_ab = ac_entry * bc_entry - ab_entry * cc_entry
    cof_ac = ab_entry * bc_entry - ac_entry * bb_entry
    cof_bb = aa_entry * cc_entry - ac_entry * ac_entry
    cof_bc = ab_entry * ac_entry - aa_entry * bc_entry
    cof_cc = aa_entry * bb_entry - ab_entry * ab_entry
    determinant = aa_entry * cof_aa + ab_entry * cof_ab + ac_entry * cof_ac
    component_a = (
        cof_aa * target[:, 0] + cof_ab * target[:, 1] + cof_ac * target[:, 2]
    ) / determinant
    component_b = (
        cof_ab * target[:, 0] + cof_bb * target[:, 1] + cof_bc * target[:, 2]
    ) / determinant
    component_c = (
        cof_ac * target[:, 0] + cof_bc * target[:, 1] + cof_cc * target[:, 2]
    ) / determinant
    return jnp.stack([component_a, component_b, component_c], axis=1)


def eliminate(cam_jac, point_jac, residual, obs_cam, camera, damping):
    cam_all = lax.all_gather(camera, "chain", axis=0, tiled=True)
    blocks, observers = obs_cam.shape
    span_width = residual.shape[2]
    per_block = span_width // observers
    gathered = cam_all[obs_cam.reshape(-1)]
    cam_values = (
        gathered.reshape(blocks, observers, 6, per_block)
        .transpose(0, 2, 1, 3)
        .reshape(blocks, 6, span_width)
    )
    cam_terms = cam_jac.astype(jnp.float32).reshape(blocks, 2, 6, span_width)
    misfit = residual + jnp.sum(cam_terms * cam_values[:, None], axis=2)
    point_terms = point_jac.astype(jnp.float32).reshape(blocks, 2, 3, observers, per_block)
    misfit_obs = misfit.reshape(blocks, 2, observers, per_block)
    unit_three = (
        lax.broadcasted_iota(jnp.int32, (3, 3), 0) == lax.broadcasted_iota(jnp.int32, (3, 3), 1)
    ).astype(jnp.float32)
    hessian = (
        jnp.sum(point_terms[:, :, :, None] * point_terms[:, :, None, :], axis=(1, 4))
        + unit_three[None, :, :, None] * damping[None, None, None, :]
    )
    target = jnp.sum(point_terms * misfit_obs[:, :, None], axis=(1, 3))
    solution = solve_three(hessian, target)
    projected = misfit_obs - jnp.sum(point_terms * solution[:, None, :, None, :], axis=2)
    adjoint = jnp.sum(cam_terms * projected.reshape(blocks, 2, 1, span_width), axis=1)
    adjoint = (
        adjoint.reshape(blocks, 6, observers, per_block)
        .transpose(0, 2, 1, 3)
        .reshape(blocks * observers, 6 * per_block)
    )
    return (adjoint, solution)


def compose_ahead(product, panels):
    inverse_block, coupling_block = panels
    step_map = -jnp.dot(coupling_block.T, inverse_block.T, preferred_element_type=jnp.float32)
    return (jnp.dot(step_map, product, precision=exact_mode), None)


def compose_back(product, panels):
    inverse_block, coupling_block = panels
    step_map = -jnp.dot(inverse_block, coupling_block, preferred_element_type=jnp.float32)
    return (jnp.dot(step_map, product, precision=exact_mode), None)


def sweep_ahead(gradient, state_in, diag_inverse, coupling):

    def advance(carried, panels):
        inverse_block, coupling_block, grad_block = panels
        inverse_wide = inverse_block.astype(jnp.float32)
        coupling_wide = coupling_block.astype(jnp.float32)
        solved = jnp.dot(inverse_wide.T, grad_block - carried, precision=exact_mode)
        return (jnp.dot(coupling_wide.T, solved, precision=exact_mode), solved)

    return lax.scan(advance, state_in, (diag_inverse, coupling, gradient))


def sweep_back(solved_all, state_in, diag_inverse, coupling):

    def retreat(later, panels):
        inverse_block, coupling_block, solved_block = panels
        inverse_wide = inverse_block.astype(jnp.float32)
        coupling_wide = coupling_block.astype(jnp.float32)
        update = jnp.dot(
            inverse_wide,
            solved_block - jnp.dot(coupling_wide, later, precision=exact_mode),
            precision=exact_mode,
        )
        return (update, update)

    return lax.scan(retreat, state_in, (diag_inverse, coupling, solved_all), reverse=True)


def join_maps(earlier, later):
    return (
        jnp.dot(later[0], earlier[0], precision=exact_mode),
        jnp.dot(later[0], earlier[1], precision=exact_mode) + later[1],
    )


def carry_across(transfer, offset, backward):
    cam_width = offset.shape[0]
    unit = (
        lax.broadcasted_iota(jnp.int32, (cam_width, cam_width), 0)
        == lax.broadcasted_iota(jnp.int32, (cam_width, cam_width), 1)
    ).astype(jnp.float32)
    zero_vec = jnp.zeros((cam_width,), jnp.float32)
    if backward:
        _, incoming = entering((transfer, offset), "chain", join_maps, (unit, zero_vec), True)
    else:
        _, incoming = entering((transfer, offset), "chain", join_maps, (unit, zero_vec), False)
    return incoming


def shards(cam_jac, point_jac, residual, obs_cam, damp_exp, cam_step, diag_inverse, coupling):
    chain_size = lax.axis_size("chain")
    local_blocks, cam_width = cam_step.shape
    total_blocks = local_blocks * chain_size
    flat_ids = obs_cam.reshape(-1)
    dampings = jnp.exp2(damp_exp.astype(jnp.float32))
    zero_vec = jnp.zeros((cam_width,), jnp.float32)
    unit = (
        lax.broadcasted_iota(jnp.int32, (cam_width, cam_width), 0)
        == lax.broadcasted_iota(jnp.int32, (cam_width, cam_width), 1)
    ).astype(jnp.float32)
    ahead_map, _ = lax.scan(compose_ahead, unit, (diag_inverse, coupling))
    back_map, _ = lax.scan(compose_back, unit, (diag_inverse, coupling), reverse=True)
    camera = cam_step
    for iteration in range(ITERS):
        damp_row = dampings[iteration]
        adjoint, _ = eliminate(cam_jac, point_jac, residual, obs_cam, camera, damp_row)
        dense_sums = jax.ops.segment_sum(adjoint, flat_ids, num_segments=total_blocks)
        partial_grad = lax.psum_scatter(dense_sums, "chain", scatter_dimension=0, tiled=True)
        cam_damp = jnp.tile(damp_row, 6)
        gradient = lax.psum(partial_grad, "pts") + cam_damp[None, :] * camera
        head_state, _ = sweep_ahead(gradient, zero_vec, diag_inverse, coupling)
        incoming = carry_across(ahead_map, head_state, False)
        _, solved_all = sweep_ahead(gradient, incoming, diag_inverse, coupling)
        tail_state, _ = sweep_back(solved_all, zero_vec, diag_inverse, coupling)
        incoming_back = carry_across(back_map, tail_state, True)
        _, update = sweep_back(solved_all, incoming_back, diag_inverse, coupling)
        camera = camera - update
    _, solution = eliminate(cam_jac, point_jac, residual, obs_cam, camera, dampings[ITERS - 1])
    return (camera, -solution)


def solution(mesh):
    in_specs = (
        P(("chain", "pts"), None, None),
        P(("chain", "pts"), None, None),
        P(("chain", "pts"), None, None),
        P(("chain", "pts"), None),
        P(),
        P("chain", None),
        P("chain", None, None),
        P("chain", None, None),
    )
    out_specs = (P("chain", None), P(("chain", "pts"), None, None))
    return jax.shard_map(shards, mesh=mesh, in_specs=in_specs, out_specs=out_specs, check_vma=False)
```

profile of v0, /device:TPU:0, one launch (start us, length us, event | category | flops | bytes accessed | tf_op | source)
XLA Modules:
  0.0 719.6 jit_solution(13044089286336931081)
XLA Ops:
  11.7 32.3 %all_gather.53 = f32[64,384]{1,0:T(8,128)S(1)} all-gather(f32[8,384]{1,0:T(8,128)S(1)} %copy-done.15), channel_id=1, replica_groups=mesh['chain'=8,'pts'=4] {'chain'}, dimensions={0}, use_global_device_ids=true | all-gather | bytes 110592 | tf_op jit(solution)/shard_map/all_gather | solution.py:55
  47.4 3.1 copy.67
  56.0 2.3 copy.72
  58.3 2.1 reshape.707
  60.4 4.2 scatter_custom_fusion
  64.9 21.7 %while.189 = (s32[]{:T(128)}, f32[384,384]{1,0:T(8,128)S(1)}, bf16[8,384,384]{2,1,0:T(8,128)(2,1)S(1)}, bf16[8,384,384]{2,1,0:T(8,128)(2,1)}, s32[]{:T(128)}) while((s32[]{:T(128)}, f32[384,384]{1,0:T(8,128)S(1)}, bf16[8,384,384]{2,1,0:T(8,128)(2,1)S(1)}, bf16[8,384,384]{2,1,0:T(8,128)(2,1)}, s32[]{:T(128)}) %tuple.412), condition=%wide.region_3.4_spmd, body=%wide.region_2.3_spmd.sunk | while | flops 792870912 | bytes 4129853 | solution.py:160
  87.5 21.1 %while.188 = (s32[]{:T(128)}, f32[384,384]{1,0:T(8,128)S(1)}, bf16[8,384,384]{2,1,0:T(8,128)(2,1)}, bf16[8,384,384]{2,1,0:T(8,128)(2,1)S(1)}, s32[]{:T(128)}, /*index=5*/s32[]{:T(128)}) while((s32[]{:T(128)}, f32[384,384]{1,0:T(8,128)S(1)}, bf16[8,384,384]{2,1,0:T(8,128)(2,1)}, bf16[8,384,384]{2,1,0:T(8,128)(2,1)S(1)}, s32[]{:T(128)}, ...), condition=%wide.region_1.2_spmd, body=%wide.region_0.1_spmd.sunk | while | flops 792870912 | bytes 4129873 | solution.py:161
  110.9 24.2 %all-reduce.5.cloned.1.call-done = f32[64,384]{1,0:T(8,128)} async-done(((f32[64,384]{1,0:T(8,128)}), f32[64,384]{1,0:T(8,128)}) %all-reduce.5.cloned.1.call-update) | async-done | bytes 98320
  135.8 10.1 %psum.14 = f32[8,384]{1,0:T(8,128)S(1)} all-reduce(f32[8,384]{1,0:T(8,128)S(1)} %constant_dynamic-slice_fusion.1), channel_id=1, replica_groups=mesh['chain'=8,'pts'=4] {'pts'}, use_global_device_ids=true, to_apply=%region_11.12 | all-reduce | flops 3072 | bytes 24576 | tf_op jit(solution)/shard_map/psum | solution.py:169
  145.9 12.3 %while.190 = (s32[]{:T(128)}, f32[384]{0:T(512)S(1)}, bf16[8,384,384]{2,1,0:T(8,128)(2,1)S(1)}, bf16[8,384,384]{2,1,0:T(8,128)(2,1)}, f32[8,384]{1,0:T(8,128)S(1)}, /*index=5*/s32[]{:T(128)}) while((s32[]{:T(128)}, f32[384]{0:T(512)S(1)}, bf16[8,384,384]{2,1,0:T(8,128)(2,1)S(1)}, bf16[8,384,384]{2,1,0:T(8,128)(2,1)}, ...), condition=%wide.region_13.14_spmd, body=%wide.region_12.13_spmd.sunk | while | flops 3539330 | bytes 607309 | solution.py:109
  158.3 26.3 %all-gather.6 = f32[8,1,384]{2,1,0:T(1,128)S(1)} all-gather(f32[1,1,384]{2,1,0:T(1,128)S(1)} %reshape.727), channel_id=4, replica_groups=mesh['chain'=8,'pts'=4] {'chain'}, dimensions={0}, use_global_device_ids=true | all-gather | bytes 13824 | tf_op jit(solution)/shard_map/all_gather | solution.py:14
  184.5 31.9 %all-gather.15.cloned.1.call-done = f32[3072,384]{1,0:T(8,128)} async-done(((f32[384,384]{1,0:T(8,128)}), f32[3072,384]{1,0:T(8,128)}) %all-gather.15.cloned.1.call-update) | async-done | bytes 4718608 | tf_op jit(solution)/shard_map/all_gather | solution.py:14
  216.4 14.6 %while.198 = (s32[]{:T(128)}, f32[384]{0:T(512)S(1)}, s32[]{:T(128)}, f32[8,384,384]{2,1,0:T(8,128)}, f32[8,384]{1,0:T(8,128)S(1)}, /*index=5*/s32[]{:T(128)}, s32[]{:T(128)}) while((s32[]{:T(128)}, f32[384]{0:T(512)S(1)}, s32[]{:T(128)}, f32[8,384,384]{2,1,0:T(8,128)}, f32[8,384]{1,0:T(8,128)S(1)}, /*index=5*/s32[]{:T(128)}, ...), condition=%wide.region_15.16_spmd.clone, body=%wide.region_14.15_spmd.clone.sunk | while | flops 1771012 | bytes 608870 | solution.py:25
  231.0 12.8 %while.191 = (s32[]{:T(128)}, f32[384]{0:T(512)S(1)}, f32[8,384]{1,0:T(8,128)S(1)}, bf16[8,384,384]{2,1,0:T(8,128)(2,1)S(1)}, bf16[8,384,384]{2,1,0:T(8,128)(2,1...) while((s32[]{:T(128)}, f32[384]{0:T(512)S(1)}, f32[8,384]{1,0:T(8,128)S(1)}, ...), condition=%wide.region_17.18_spmd, body=%wide.region_16.17_spmd.sunk | while | flops 3539330 | bytes 610401 | solution.py:109
  243.8 14.6 %while.192 = (s32[]{:T(128)}, f32[384]{0:T(512)S(1)}, bf16[8,384,384]{2,1,0:T(8,128)(2,1)}, f32[8,384]{1,0:T(8,128)S(1)}, bf16[8,384,384]{2,1,0:T(8,128)(2,1)S(1)}, /*index=5*/s32[]{:T(128)}, s32[]{:T(128)}) while((s32[]{:T(128)}, f32[384]{0:T(512)S(1)}, bf16[8,384,384]{2,1,0:T(8,128)(2,1)}, f32[8,384]{1,0:T(8,128)S(1)}, ...), condition=%wide.region_19.20_spmd, body=%wide.region_18.19_spmd.sunk | while | flops 3539331 | bytes 609893 | solution.py:125
  258.4 26.5 %all-gather.7 = f32[8,1,384]{2,1,0:T(1,128)S(1)} all-gather(f32[1,1,384]{2,1,0:T(1,128)S(1)} %reshape.729), channel_id=5, replica_groups=mesh['chain'=8,'pts'=4] {'chain'}, dimensions={0}, use_global_device_ids=true | all-gather | bytes 13824 | tf_op jit(solution)/shard_map/all_gather | solution.py:14
  284.9 12.2 %all-gather.13.cloned.1.call-done = f32[3072,384]{1,0:T(8,128)} async-done(((f32[384,384]{1,0:T(8,128)}), f32[3072,384]{1,0:T(8,128)}) %all-gather.13.cloned.1.call-update) | async-done | bytes 4718608 | tf_op jit(solution)/shard_map/all_gather | solution.py:14
  297.1 14.5 %while.199 = (s32[]{:T(128)}, f32[384]{0:T(512)S(1)}, s32[]{:T(128)}, f32[8,384,384]{2,1,0:T(8,128)}, f32[8,384]{1,0:T(8,128)S(1)}, /*index=5*/s32[]{:T(128)}, s32[]{:T(128)}, s32[]{:T(128)}, s32[]{:T(128)}) while((s32[]{:T(128)}, f32[384]{0:T(512)S(1)}, s32[]{:T(128)}, f32[8,384,384]{2,1,0:T(8,128)}, f32[8,384]{1,0:T(8,128)S(1)}, ...), condition=%wide.region_21.22_spmd.clone, body=%wide.region_20.21_spmd.clone.sunk | while | flops 1771016 | bytes 608424 | solution.py:25
  311.7 15.0 %while.193 = (s32[]{:T(128)}, f32[384]{0:T(512)S(1)}, f32[8,384]{1,0:T(8,128)S(1)}, bf16[8,384,384]{2,1,0:T(8,128)(2,1)}, f32[8,384]{1,0:T(8,128)S(1)}, /*index=...) while((s32[]{:T(128)}, f32[384]{0:T(512)S(1)}, f32[8,384]{1,0:T(8,128)S(1)}, ...), condition=%wide.region_23.24_spmd, body=%wide.region_22.23_spmd.sunk | while | flops 3539331 | bytes 614521 | solution.py:125
  327.3 30.8 %all_gather.58 = f32[64,384]{1,0:T(8,128)S(1)} all-gather(f32[8,384]{1,0:T(8,128)S(1)} %sub.297), channel_id=1, replica_groups=mesh['chain'=8,'pts'=4] {'chain'}, dimensions={0}, use_global_device_ids=true | all-gather | bytes 110592 | tf_op jit(solution)/shard_map/all_gather | solution.py:55
  361.4 3.1 copy.73
  364.5 2.6 mul.764
  372.1 2.0 multiply_reduce_fusion.3
  380.4 2.5 reshape.672
  382.9 3.7 copy.76
  386.6 2.7 reshape.715
  389.3 4.8 scatter_custom_fusion.1
  394.2 67.4 %all-reduce.7.cloned.1.call-done = f32[64,384]{1,0:T(8,128)} async-done(((f32[64,384]{1,0:T(8,128)}), f32[64,384]{1,0:T(8,128)}) %all-reduce.7.cloned.1.call-update) | async-done | bytes 98320
  462.9 11.2 %psum.15 = f32[8,384]{1,0:T(8,128)} all-reduce(f32[8,384]{1,0:T(8,128)} %constant_dynamic-slice_fusion), channel_id=1, replica_groups=mesh['chain'=8,'pts'=4] {'pts'}, use_global_device_ids=true, to_apply=%region_30.31 | all-reduce | flops 3072 | bytes 24576 | tf_op jit(solution)/shard_map/psum | solution.py:169
  475.4 17.9 %while.194 = (s32[]{:T(128)}, f32[384]{0:T(512)S(1)}, bf16[8,384,384]{2,1,0:T(8,128)(2,1)S(1)}, bf16[8,384,384]{2,1,0:T(8,128)(2,1)}, f32[8,384]{1,0:T(8,128)}, /*index=5*/s32[]{:T(128)}) while((s32[]{:T(128)}, f32[384]{0:T(512)S(1)}, bf16[8,384,384]{2,1,0:T(8,128)(2,1)S(1)}, bf16[8,384,384]{2,1,0:T(8,128)(2,1)}, f32[8,384]{1,0:T(8,128)}, ...), condition=%wide.region_32.33_spmd, body=%wide.region_31.32_spmd.sunk | while | flops 3539330 | bytes 607309 | solution.py:109
  493.4 25.9 %all-gather.8 = f32[8,1,384]{2,1,0:T(1,128)S(1)} all-gather(f32[1,1,384]{2,1,0:T(1,128)S(1)} %reshape.731), channel_id=6, replica_groups=mesh['chain'=8,'pts'=4] {'chain'}, dimensions={0}, use_global_device_ids=true | all-gather | bytes 13824 | tf_op jit(solution)/shard_map/all_gather | solution.py:14
  519.9 20.1 %while.200 = (s32[]{:T(128)}, f32[384]{0:T(512)S(1)}, s32[]{:T(128)}, f32[8,384,384]{2,1,0:T(8,128)}, f32[8,384]{1,0:T(8,128)}, /*index=5*/s32[]{:T(128)}, s32[]{:T(128)}) while((s32[]{:T(128)}, f32[384]{0:T(512)S(1)}, s32[]{:T(128)}, f32[8,384,384]{2,1,0:T(8,128)}, f32[8,384]{1,0:T(8,128)}, /*index=5*/s32[]{:T(128)}, ...), condition=%wide.region_34.35_spmd.clone, body=%wide.region_33.34_spmd.clone.sunk | while | flops 1771012 | bytes 608870 | solution.py:25
  540.6 28.4 %while.195 = (s32[]{:T(128)}, f32[384]{0:T(512)S(1)}, f32[8,384]{1,0:T(8,128)}, bf16[8,384,384]{2,1,0:T(8,128)(2,1)S(1)}, bf16[8,384,384]{2,1,0:T(8,128)(2,1)}, /*index=5*/f32[8,384]{1,0:T(8,128)}, s32[]{:T(128)}, s32[]{:T(128)}) while((s32[]{:T(128)}, f32[384]{0:T(512)S(1)}, f32[8,384]{1,0:T(8,128)}, bf16[8,384,384]{2,1,0:T(8,128)(2,1)S(1)}, ...), condition=%wide.region_36.37_spmd, body=%wide.region_35.36_spmd.sunk | while | flops 3539330 | bytes 610401 | solution.py:109
  569.0 20.2 %while.196 = (s32[]{:T(128)}, f32[384]{0:T(512)S(1)}, bf16[8,384,384]{2,1,0:T(8,128)(2,1)}, f32[8,384]{1,0:T(8,128)}, bf16[8,384,384]{2,1,0:T(8,128)(2,1)S(1)}, /*index=5*/s32[]{:T(128)}, s32[]{:T(128)}) while((s32[]{:T(128)}, f32[384]{0:T(512)S(1)}, bf16[8,384,384]{2,1,0:T(8,128)(2,1)}, f32[8,384]{1,0:T(8,128)}, ...), condition=%wide.region_38.39_spmd, body=%wide.region_37.38_spmd.sunk | while | flops 3539331 | bytes 609893 | solution.py:125
  589.2 25.9 %all-gather.9 = f32[8,1,384]{2,1,0:T(1,128)S(1)} all-gather(f32[1,1,384]{2,1,0:T(1,128)S(1)} %reshape.733), channel_id=7, replica_groups=mesh['chain'=8,'pts'=4] {'chain'}, dimensions={0}, use_global_device_ids=true | all-gather | bytes 13824 | tf_op jit(solution)/shard_map/all_gather | solution.py:14
  615.7 20.2 %while.201 = (s32[]{:T(128)}, f32[384]{0:T(512)S(1)}, s32[]{:T(128)}, f32[8,384,384]{2,1,0:T(8,128)}, f32[8,384]{1,0:T(8,128)}, /*index=5*/s32[]{:T(128)}, s32[]{:T(128)}, s32[]{:T(128)}, s32[]{:T(128)}) while((s32[]{:T(128)}, f32[384]{0:T(512)S(1)}, s32[]{:T(128)}, f32[8,384,384]{2,1,0:T(8,128)}, f32[8,384]{1,0:T(8,128)}, ...), condition=%wide.region_40.41_spmd.clone, body=%wide.region_39.40_spmd.clone.sunk | while | flops 1771016 | bytes 608424 | solution.py:25
  636.5 35.3 %while.197 = (s32[]{:T(128)}, f32[384]{0:T(512)S(1)}, f32[8,384]{1,0:T(8,128)}, bf16[8,384,384]{2,1,0:T(8,128)(2,1)}, f32[8,384]{1,0:T(8,128)}, /*index=5*/bf16[...) while((s32[]{:T(128)}, f32[384]{0:T(512)S(1)}, f32[8,384]{1,0:T(8,128)}, ...), condition=%wide.region_42.43_spmd, body=%wide.region_41.42_spmd.sunk | while | flops 3539331 | bytes 614521 | solution.py:125
  637.6 1.9 fusion.209
  642.0 1.9 fusion.209
  646.5 1.9 fusion.209
  650.9 1.9 fusion.209
  655.3 1.9 fusion.209
  659.7 1.9 fusion.209
  664.1 1.9 fusion.209
  668.5 1.9 fusion.209
  672.5 30.8 %all_gather.63 = f32[64,384]{1,0:T(8,128)S(1)} all-gather(f32[8,384]{1,0:T(8,128)S(1)} %sub.305), channel_id=1, replica_groups=mesh['chain'=8,'pts'=4] {'chain'}, dimensions={0}, use_global_device_ids=true | all-gather | bytes 110592 | tf_op jit(solution)/shard_map/all_gather | solution.py:55
  703.3 2.4 gather_fusion.2
  708.7 1.9 mul.804
  (724 shorter events, 293.3 us)
Async XLA Ops:
  7.2 4.4 copy-start.23
  7.2 4.5 copy-start.15
  7.2 127.9 %all-reduce.5.cloned.1.call-start = ((), (), s32[]{:S(2)}) async-start(), calls=%async_computation.2 | async-start | bytes 196608
  8.2 52.2 %copy-start.22 = (s32[512]{0:T(512)}, s32[512]{0:T(512)S(1)}, u32[]{:S(2)}) copy-start(s32[512]{0:T(512)S(1)} %reshape.705) | copy-start | bytes 6148
  9.7 45.4 %copy-start.1 = (f32[64,2,3,8,64]{4,3,0,2,1:T(8,128)}, f32[64,2,3,8,64]{4,3,0,2,1:T(8,128)S(1)}, u32[]{:S(2)}) copy-start(f32[64,2,3,8,64]{4,3,0,2,1:T(8,128)S(1)} %reshape.678) | copy-start | bytes 2359300
  11.6 41.5 %copy-start.18 = (f32[64]{0:T(128)}, f32[64]{0:T(128)S(1)}, u32[]{:S(2)}) copy-start(f32[64]{0:T(128)S(1)} %get-tuple-element.1381) | copy-start | bytes 772
  11.6 41.5 %copy-start.20 = (f32[64]{0:T(128)}, f32[64]{0:T(128)S(1)}, u32[]{:S(2)}) copy-start(f32[64]{0:T(128)S(1)} %get-tuple-element.1382) | copy-start | bytes 772
  11.7 346.4 %copy-start.17 = (s32[1024]{0:T(1024)}, s32[1024]{0:T(1024)S(1)}, u32[]{:S(2)}) copy-start(s32[1024]{0:T(1024)S(1)} %pad_clamp_fusion) | copy-start | bytes 12292
  47.4 5.0 copy-start.6
  50.5 2.1 copy-start.9
  58.3 6.6 copy-start
  64.6 151.8 %all-gather.15.cloned.1.call-start = ((), (), s32[]{:S(2)}) async-start(), calls=%async_computation.1 | async-start | bytes 5308416 | tf_op jit(solution)/shard_map/all_gather | solution.py:14
  86.6 0.8 copy-start.5
  87.4 209.7 %all-gather.13.cloned.1.call-start = ((), (), s32[]{:S(2)}) async-start(), calls=%async_computation | async-start | bytes 5308416 | tf_op jit(solution)/shard_map/all_gather | solution.py:14
  87.5 22.1 %copy-start.21 = (f32[64]{0:T(128)S(1)}, f32[64]{0:T(128)}, u32[]{:S(2)}) copy-start(f32[64]{0:T(128)} %copy-done.20) | copy-start | bytes 772
  87.5 22.2 %copy-start.24 = (u32[32]{0:T(128)S(1)}, u32[32]{0:T(128)}, u32[]{:S(2)}) copy-start(u32[32]{0:T(128)} %constant.373) | copy-start | bytes 388
  108.6 0.8 copy-start.4
  109.4 352.1 %all-reduce.7.cloned.1.call-start = ((), (), s32[]{:S(2)}) async-start(), calls=%async_computation.3 | async-start | bytes 196608
  326.7 0.6 copy-start.12
  361.4 5.7 copy-start.7
  367.1 7.0 copy-start.8
  372.1 3.2 copy-start.2
  374.7 0.6 copy-start.10
  386.6 7.5 %copy-start.19 = (f32[64]{0:T(128)S(1)}, f32[64]{0:T(128)}, u32[]{:S(2)}) copy-start(f32[64]{0:T(128)} %copy-done.18) | copy-start | bytes 772
  635.9 35.9 %copy-start.13 = (f32[8,384]{1,0:T(8,128)S(1)}, f32[8,384]{1,0:T(8,128)}, u32[]{:S(2)}) copy-start(f32[8,384]{1,0:T(8,128)} %copy-done.12) | copy-start | bytes 36868
  672.5 30.8 %copy-start.16 = (f32[8,384]{1,0:T(8,128)}, f32[8,384]{1,0:T(8,128)S(1)}, u32[]{:S(2)}) copy-start(f32[8,384]{1,0:T(8,128)S(1)} %sub.305) | copy-start | bytes 36868
  708.7 3.3 copy-start.3
  710.8 1.5 copy-start.11
  710.9 1.6 copy-start.14
Sparse Core Ops, SparseCore 0:
  64.7 70.3 all-reduce.4
  137.3 79.0 all-gather.14
  218.6 78.4 all-gather.12
  394.2 67.3 all-reduce.6
where the time goes:
time: 728 us; the launch traced here: 720 us
  blocking collectives  220 us (30%)
  matrix products  206 us (28%)
  waiting for transfers between devices  136 us (19%)
  local copies, waits for them, and re-layouts  112 us (15%)
  other arithmetic  27.9 us (4%)
  between operations  15 us (2%)
    all_gather x4, blocking collectives, entering(): everything = jax.tree.map(lambda part: lax.all_gather(part, axis), x)  105 us
    all_gather x3, blocking collectives, eliminate(): cam_all = lax.all_gather(camera, 'chain', axis=0, tiled=True)  93.9 us
    unnamed x6, waiting for transfers between devices  91.6 us
    dot_general x32, matrix products, join_maps(): jnp.dot(later[0], earlier[1], precision=exact_mode) + later[1]  55.3 us
    dot_general x32, matrix products, retreat(): jnp.dot(inverse_wide, solved_block - jnp.dot(coupling_wide, later, precis...  48.2 us
    all_gather x2, waiting for transfers between devices, entering(): everything = jax.tree.map(lambda part: lax.all_gather(part, axis), x)  44.1 us
    dot_general x32, matrix products, advance(): solved = jnp.dot(inverse_wide.T, grad_block - carried, precision=exact_mode)  38.6 us
    dynamic_slice x64, local copies, waits for them, and re-layouts, sweep_ahead(): return lax.scan(advance, state_in, (diag_inverse, coupling, gradient))  24.1 us
  transfers between devices with their start and end apart: 4, of which 4 were waited for; matrix products, arithmetic and copies ran while one was open for 14% of the time, Pallas kernels for 0%

commit v1 on v0

v1 whole, which is shorter than its diff:
```python
import functools

import jax
import jax.numpy as jnp
from jax import lax
from jax.experimental import pallas as pl
from jax.experimental.pallas import tpu as pltpu
from jax.sharding import PartitionSpec as P

ITERS = 2
MESH = pl.DeviceIdType.MESH
F32, BF16 = jnp.float32, jnp.bfloat16
VMEM = pl.BlockSpec(memory_space=pltpu.VMEM)
ANY = pl.BlockSpec(memory_space=pl.ANY)


def dot_rows(x, panel):
    return lax.dot_general(x, panel, (((1,), (0,)), ((), ())), preferred_element_type=F32)


def dot_cols(x, panel):
    return lax.dot_general(x, panel, (((1,), (1,)), ((), ())), preferred_element_type=F32)


def halves(x):
    high = x.astype(BF16)
    return high, (x - high.astype(F32)).astype(BF16)


def thirds(x):
    high = x.astype(BF16)
    rest = x - high.astype(F32)
    mid = rest.astype(BF16)
    return high, mid, (rest - mid.astype(F32)).astype(BF16)


def maps_kernel(
    df_ref, cf_ref, db_ref, cb_ref, wh_ref, wl_ref, xh_ref, xl_ref, rh_ref, rl_ref, run_f, run_b
):
    @pl.when(pl.program_id(0) == 0)
    def _():
        width = run_f.shape[0]
        unit = (
            lax.broadcasted_iota(jnp.int32, (width, width), 0)
            == lax.broadcasted_iota(jnp.int32, (width, width), 1)
        ).astype(F32)
        run_f[...] = unit
        run_b[...] = unit

    high, low = halves(run_f[...])
    solved = -(dot_rows(high, df_ref[0]) + dot_rows(low, df_ref[0]))
    high, low = halves(solved)
    wh_ref[0] = high
    wl_ref[0] = low
    run_f[...] = dot_rows(high, cf_ref[0]) + dot_rows(low, cf_ref[0])
    high, low = halves(run_b[...])
    misfit = -(dot_cols(high, cb_ref[0]) + dot_cols(low, cb_ref[0]))
    high, low = halves(misfit)
    update = dot_cols(high, db_ref[0]) + dot_cols(low, db_ref[0])
    run_b[...] = update
    high, low = halves(update)
    xh_ref[0] = high
    xl_ref[0] = low

    @pl.when(pl.program_id(0) == pl.num_programs(0) - 1)
    def _():
        high, low = halves(run_f[...])
        rh_ref[...] = high
        rl_ref[...] = low


def sweep_maps(diag_inverse, coupling):
    count, width, _ = diag_inverse.shape
    ahead = pl.BlockSpec((1, width, width), lambda k: (k, 0, 0))
    back = pl.BlockSpec((1, width, width), lambda k: (count - 1 - k, 0, 0))
    whole = pl.BlockSpec((width, width), lambda k: (0, 0))
    stack = jax.ShapeDtypeStruct((count, width, width), BF16)
    one = jax.ShapeDtypeStruct((width, width), BF16)
    return pl.pallas_call(
        maps_kernel,
        grid=(count,),
        in_specs=[ahead, ahead, back, back],
        out_specs=[ahead, ahead, back, back, whole, whole],
        out_shape=[stack, stack, stack, stack, one, one],
        scratch_shapes=[pltpu.VMEM((width, width), F32)] * 2,
        compiler_params=pltpu.CompilerParams(vmem_limit_bytes=32 << 20),
        name="sweep_maps",
    )(diag_inverse, coupling, diag_inverse, coupling)


def eliminate_kernel(adjoint_out, *refs):
    if adjoint_out:
        cam_ref, pick_ref, pick_t_ref, cj_ref, pj_ref, res_ref, damp_ref, out_ref, seen, parts = refs
    else:
        cam_ref, pick_ref, cj_ref, pj_ref, res_ref, damp_ref, out_ref, seen = refs
    rows = res_ref.shape[1]
    blocks = rows // 4
    high, mid, low = thirds(cam_ref[...])
    pick = pick_ref[...]
    seen[...] = (dot_rows(pick, low) + dot_rows(pick, mid)) + dot_rows(pick, high)
    step = 16
    left = lax.broadcasted_iota(jnp.int32, (step, 128), 1) < 64
    damp = damp_ref[...]

    def swap(x):
        return pltpu.roll(x, 64, 1)

    def chunk(i, carry):
        at = pl.multiple_of(i * step, step)
        misfits, points = [], []
        hess = [None] * 6
        target = [None] * 3
        pairs = ((0, 0), (0, 1), (0, 2), (1, 1), (1, 2), (2, 2))
        for tp in range(4):
            here = pl.ds(tp * blocks + at, step)
            there = pl.ds(rows + tp * blocks + at, step)
            cams = []
            for c in range(3):
                even = seen[here, c * 128 : (c + 1) * 128]
                odd = seen[there, c * 128 : (c + 1) * 128]
                cams.append(jnp.where(left, even, swap(odd)))
                cams.append(jnp.where(left, swap(even), odd))
            for a in range(2):
                miss = res_ref[a, here, :]
                for m in range(6):
                    miss = miss + cj_ref[6 * a + m, here, :].astype(F32) * cams[m]
                terms = [pj_ref[3 * a + n, here, :].astype(F32) for n in range(3)]
                misfits.append(miss)
                points.append(terms)
                for e, (n, k) in enumerate(pairs):
                    new = terms[n] * terms[k]
                    hess[e] = new if hess[e] is None else hess[e] + new
                for n in range(3):
                    new = terms[n] * miss
                    target[n] = new if target[n] is None else target[n] + new
        hess = [h + swap(h) for h in hess]
        ta, tb, tc = [t + swap(t) for t in target]
        aa, ab, ac, bb, bc, cc = hess
        aa, bb, cc = aa + damp, bb + damp, cc + damp
        cof_aa = bb * cc - bc * bc
        cof_ab = ac * bc - ab * cc
        cof_ac = ab * bc - ac * bb
        cof_bb = aa * cc - ac * ac
        cof_bc = ab * ac - aa * bc
        cof_cc = aa * bb - ab * ab
        det = aa * cof_aa + ab * cof_ab + ac * cof_ac
        sol = (
            (cof_aa * ta + cof_ab * tb + cof_ac * tc) / det,
            (cof_ab * ta + cof_bb * tb + cof_bc * tc) / det,
            (cof_ac * ta + cof_bc * tb + cof_cc * tc) / det,
        )
        if not adjoint_out:
            for n in range(3):
                out_ref[n, pl.ds(at, step), :] = -sol[n]
            return carry
        for tp in range(4):
            here = pl.ds(tp * blocks + at, step)
            there = pl.ds(rows + tp * blocks + at, step)
            left_over = []
            for a in range(2):
                terms = points[2 * tp + a]
                left_over.append(
                    misfits[2 * tp + a]
                    - (terms[0] * sol[0] + terms[1] * sol[1] + terms[2] * sol[2])
                )
            adj = [
                cj_ref[m, here, :].astype(F32) * left_over[0]
                + cj_ref[6 + m, here, :].astype(F32) * left_over[1]
                for m in range(6)
            ]
            for c in range(3):
                span = slice(c * 128, (c + 1) * 128)
                even = jnp.where(left, adj[2 * c], swap(adj[2 * c + 1]))
                odd = jnp.where(left, swap(adj[2 * c]), adj[2 * c + 1])
                for part, value in enumerate(thirds(even)):
                    parts[part, here, span] = value
                for part, value in enumerate(thirds(odd)):
                    parts[part, there, span] = value
        return carry

    lax.fori_loop(0, blocks // step, chunk, 0)
    if adjoint_out:
        pick_t = pick_t_ref[...]
        out_ref[...] = (
            dot_rows(pick_t, parts[2]) + dot_rows(pick_t, parts[1])
        ) + dot_rows(pick_t, parts[0])


def eliminate(cam_all, pick, pick_t, cj, pj, res, damp, adjoint_out):
    rows, width = res.shape[1], cam_all.shape[1]
    scratch = [pltpu.VMEM((2 * rows, width), F32)]
    if adjoint_out:
        args = (cam_all, pick, pick_t, cj, pj, res, damp)
        out = jax.ShapeDtypeStruct(cam_all.shape, F32)
        scratch.append(pltpu.VMEM((3, 2 * rows, width), BF16))
    else:
        args = (cam_all, pick, cj, pj, res, damp)
        out = jax.ShapeDtypeStruct((3, rows // 4, 128), F32)
    return pl.pallas_call(
        functools.partial(eliminate_kernel, adjoint_out),
        in_specs=[VMEM] * len(args),
        out_specs=VMEM,
        out_shape=out,
        scratch_shapes=scratch,
        compiler_params=pltpu.CompilerParams(vmem_limit_bytes=40 << 20),
        name="eliminate",
    )(*args)


def split_row(v):
    row = lax.broadcasted_iota(jnp.int32, v.shape, 0)
    high = v.astype(BF16).astype(F32)
    rest = v - high
    mid = rest.astype(BF16).astype(F32)
    low = rest - mid
    return jnp.where(row == 0, high, jnp.where(row == 1, mid, jnp.where(row == 2, low, 0.0))).astype(BF16)


def total(y):
    return jnp.broadcast_to(jnp.sum(y, axis=0, keepdims=True), y.shape)


def times(v, panel):
    return total(dot_rows(split_row(v), panel))


def times_t(v, panel):
    return total(dot_cols(split_row(v), panel))


def solve_kernel(
    n_c, n_p,
    dense_ref, cam_ref, damp_ref, d_hbm, c_hbm, wh_hbm, wl_hbm, xh_hbm, xl_hbm, rh_ref, rl_ref,
    own_ref, all_ref,
    d_ref, c_ref, wh_ref, wl_ref, xh_ref, xl_ref,
    landed, piece, grad, solved, carry_in, carry_out, later_in, later_out,
    load_sem, rs_send, rs_recv, pts_send, pts_recv, ring_send, ring_recv, all_send, all_recv,
):
    me_c, me_p = lax.axis_index("chain"), lax.axis_index("pts")
    n = n_c * n_p
    me = me_c * n_p + me_p
    count = cam_ref.shape[0]
    share = count // n_p

    loads = [
        pltpu.make_async_copy(src, dst, load_sem.at[i])
        for i, (src, dst) in enumerate(
            ((d_hbm, d_ref), (c_hbm, c_ref), (wh_hbm, wh_ref), (wl_hbm, wl_ref), (xh_hbm, xh_ref), (xl_hbm, xl_ref))
        )
    ]
    for load in loads:
        load.start()

    barrier = pltpu.get_barrier_semaphore()

    @pl.loop(1, n)
    def _(i):
        to = lax.rem(me + i, n)
        pl.semaphore_signal(
            barrier, inc=1, device_id=(to // n_p, lax.rem(to, n_p)), device_id_type=MESH
        )

    pl.semaphore_wait(barrier, n - 1)

    def rs_copy(i):
        to = lax.rem(me + i, n)
        return pltpu.make_async_remote_copy(
            src_ref=dense_ref.at[to],
            dst_ref=landed.at[i],
            send_sem=rs_send.at[i],
            recv_sem=rs_recv.at[i],
            device_id=(to // n_p, lax.rem(to, n_p)),
            device_id_type=MESH,
        )

    @pl.loop(1, n)
    def _(i):
        rs_copy(i).start()

    landed[0] = dense_ref[me]

    @pl.loop(1, n)
    def _(i):
        rs_copy(i).wait_recv()

    piece[...] = jnp.sum(landed[...], axis=0)

    def pts_copy(i):
        return pltpu.make_async_remote_copy(
            src_ref=piece,
            dst_ref=grad.at[me_p],
            send_sem=pts_send.at[i],
            recv_sem=pts_recv.at[i],
            device_id=(me_c, lax.rem(me_p + i, n_p)),
            device_id_type=MESH,
        )

    for i in range(1, n_p):
        pts_copy(i).start()
    grad[me_p] = piece[...]
    for i in range(1, n_p):
        pts_copy(i).wait_recv()

    damp = damp_ref[...]
    for load in loads[:2]:
        load.wait()

    carried = None
    shape = carry_in.shape
    for k in range(count):
        g = grad[k // share, k % share : k % share + 1, :] + damp * cam_ref[k : k + 1, :]
        g = jnp.broadcast_to(g, shape)
        s = times(g if carried is None else g - carried, d_ref[k])
        solved[k : k + 1, :] = s[0:1]
        carried = times(s, c_ref[k])

    ring_f = pltpu.make_async_remote_copy(
        src_ref=carry_out, dst_ref=carry_in, send_sem=ring_send.at[0], recv_sem=ring_recv.at[0],
        device_id=(lax.rem(me_c + 1, n_c), me_p), device_id_type=MESH,
    )

    @pl.when(me_c == 0)
    def _():
        carry_in[...] = jnp.zeros_like(carry_in)

    @pl.when(me_c > 0)
    def _():
        ring_f.wait_recv()

    x = split_row(carry_in[...])
    carry_out[...] = carried + total(dot_rows(x, rh_ref[...]) + dot_rows(x, rl_ref[...]))

    @pl.when(me_c < n_c - 1)
    def _():
        ring_f.start()

    for load in loads[2:4]:
        load.wait()
    for k in range(count):
        y = dot_rows(x, wh_ref[k]) + dot_rows(x, wl_ref[k])
        solved[k : k + 1, :] = solved[k : k + 1, :] + jnp.sum(y, axis=0, keepdims=True)

    later = None
    updates = [None] * count
    for k in reversed(range(count)):
        r = jnp.broadcast_to(solved[k : k + 1, :], shape)
        if later is not None:
            r = r - times_t(later, c_ref[k])
        later = times_t(r, d_ref[k])
        updates[k] = later[0:1]

    ring_b = pltpu.make_async_remote_copy(
        src_ref=later_out, dst_ref=later_in, send_sem=ring_send.at[1], recv_sem=ring_recv.at[1],
        device_id=(lax.rem(me_c + n_c - 1, n_c), me_p), device_id_type=MESH,
    )

    for load in loads[4:]:
        load.wait()

    @pl.when(me_c == n_c - 1)
    def _():
        later_in[...] = jnp.zeros_like(later_in)

    @pl.when(me_c < n_c - 1)
    def _():
        ring_b.wait_recv()

    x = split_row(later_in[...])
    later_out[...] = later + total(dot_rows(x, xh_ref[0]) + dot_rows(x, xl_ref[0]))

    @pl.when(me_c > 0)
    def _():
        ring_b.start()

    for k in range(count):
        y = dot_rows(x, xh_ref[k]) + dot_rows(x, xl_ref[k])
        own_ref[k : k + 1, :] = cam_ref[k : k + 1, :] - (updates[k] + jnp.sum(y, axis=0, keepdims=True))

    def all_copy(i):
        return pltpu.make_async_remote_copy(
            src_ref=own_ref,
            dst_ref=all_ref.at[me_c],
            send_sem=all_send.at[i],
            recv_sem=all_recv.at[i],
            device_id=(lax.rem(me_c + i, n_c), me_p),
            device_id_type=MESH,
        )

    @pl.loop(1, n_c)
    def _(i):
        all_copy(i).start()

    all_ref[me_c] = own_ref[...]

    @pl.loop(1, n_c)
    def _(i):
        all_copy(i).wait()

    @pl.loop(1, n)
    def _(i):
        rs_copy(i).wait_send()

    for i in range(1, n_p):
        pts_copy(i).wait_send()

    @pl.when(me_c < n_c - 1)
    def _():
        ring_f.wait_send()

    @pl.when(me_c > 0)
    def _():
        ring_b.wait_send()


def solve(n_c, n_p, dense, camera, damp, diag_inverse, coupling, maps):
    count, width = camera.shape
    n = n_c * n_p
    share = count // n_p
    wh, wl, xh, xl, rh, rl = maps
    panel = pltpu.VMEM((count, width, width), BF16)
    vec = pltpu.VMEM((8, width), F32)
    sem = pltpu.SemaphoreType.DMA
    own, everyone = pl.pallas_call(
        functools.partial(solve_kernel, n_c, n_p),
        in_specs=[VMEM, VMEM, VMEM, ANY, ANY, ANY, ANY, ANY, ANY, VMEM, VMEM],
        out_specs=[VMEM, VMEM],
        out_shape=[
            jax.ShapeDtypeStruct((count, width), F32),
            jax.ShapeDtypeStruct((n_c, count, width), F32),
        ],
        scratch_shapes=[panel] * 6
        + [
            pltpu.VMEM((n, share, width), F32),
            pltpu.VMEM((share, width), F32),
            pltpu.VMEM((n_p, share, width), F32),
            pltpu.VMEM((count, width), F32),
            vec, vec, vec, vec,
            sem((6,)), sem((n,)), sem((n,)), sem((n_p,)), sem((n_p,)),
            sem((2,)), sem((2,)), sem((n_c,)), sem((n_c,)),
        ],
        compiler_params=pltpu.CompilerParams(
            collective_id=0, has_side_effects=True, vmem_limit_bytes=40 << 20
        ),
        name="solve",
    )(dense.reshape(n, share, width), camera, damp, diag_inverse, coupling, wh, wl, xh, xl, rh, rl)
    return own, everyone.reshape(n_c * count, width)


def shards(n_c, n_p, cam_jac, point_jac, residual, obs_cam, damp_exp, cam_step, diag_inverse, coupling):
    blocks, observers = obs_cam.shape
    total_blocks = cam_step.shape[0] * n_c
    pairs = observers // 2

    def by_pair(x):
        comps = x.shape[1]
        return x.reshape(blocks, comps, pairs, 128).transpose(1, 2, 0, 3).reshape(comps, pairs * blocks, 128)

    cj, pj, res = by_pair(cam_jac), by_pair(point_jac), by_pair(residual)
    order = obs_cam.reshape(blocks, pairs, 2).transpose(2, 1, 0).reshape(-1)
    cams = lax.iota(jnp.int32, total_blocks)
    pick = (order[:, None] == cams[None, :]).astype(BF16)
    pick_t = (cams[:, None] == order[None, :]).astype(BF16)
    dampings = jnp.exp2(damp_exp.astype(F32))
    wide = jnp.tile(dampings, (1, 6))
    maps = sweep_maps(diag_inverse, coupling)
    camera = cam_step
    cam_all = lax.all_gather(camera, "chain", axis=0, tiled=True)
    for iteration in range(ITERS):
        damp = wide[iteration][None]
        dense = eliminate(cam_all, pick, pick_t, cj, pj, res, damp[:, :128], True)
        camera, cam_all = solve(n_c, n_p, dense, camera, damp, diag_inverse, coupling, maps)
    out = eliminate(cam_all, pick, pick_t, cj, pj, res, wide[ITERS - 1][None, :128], False)
    return camera, out[:, :, :64].transpose(1, 0, 2)


def solution(mesh):
    in_specs = (
        P(("chain", "pts"), None, None),
        P(("chain", "pts"), None, None),
        P(("chain", "pts"), None, None),
        P(("chain", "pts"), None),
        P(),
        P("chain", None),
        P("chain", None, None),
        P("chain", None, None),
    )
    out_specs = (P("chain", None), P(("chain", "pts"), None, None))
    inner = functools.partial(shards, mesh.shape["chain"], mesh.shape["pts"])
    return jax.shard_map(inner, mesh=mesh, in_specs=in_specs, out_specs=out_specs, check_vma=False)
```

time: 728 us -> 230 us (0.32); the launches traced: 720 us -> 229 us
  matrix products: 206 us -> 0 us
  blocking collectives: 220 us -> 32.3 us
  Pallas kernels: 0 us -> 154 us
  waiting for transfers between devices: 136 us -> 0 us
  local copies, waits for them, and re-layouts: 112 us -> 40.6 us
  other arithmetic: 27.9 us -> 2.1 us
  between operations: 15 us -> 0.86 us
    dot_general x192 -> x0, matrix products: 206 us -> none  [the longest x32 55.3 us: join_maps(): jnp.dot(later[0], earlier[1], precision=exact_mode) + later[1]]
    all_gather x7 -> x1, blocking collectives: 198 us -> 32.3 us  [shards(): cam_all = lax.all_gather(camera, 'chain', axis=0, tiled=True)]
    pallas_call x0 -> x6, Pallas kernels: none -> 154 us  [the longest x2 132 us: solve(): pl.pallas_call(functools.partial(solve_kernel, n_c, n_p), in_specs=[VMEM,...]
    unnamed x6 -> x0, waiting for transfers between devices: 91.6 us -> none
    all_gather x2 -> x0, waiting for transfers between devices: 44.1 us -> none  [entering(): everything = jax.tree.map(lambda part: lax.all_gather(part, axis), x)]
    dynamic_slice x96 -> x0, local copies, waits for them, and re-layouts: 36.2 us -> none  [the longest x64 24.1 us: sweep_ahead(): return lax.scan(advance, state_in, (diag_inverse, coupling, gradient))]
    unnamed x63 -> x81, local copies, waits for them, and re-layouts: 7.53 us -> 29.5 us
    dynamic_update_slice x32 -> x0, local copies, waits for them, and re-layouts: 21.7 us -> none  [sweep_ahead(): return lax.scan(advance, state_in, (diag_inverse, coupling, gradient))]
  transfers between devices with their start and end apart: 4 -> 0, of which waited for: 4 -> 0; matrix products, arithmetic and copies ran while one was open for 14% -> 0% of each run, Pallas kernels for 0% -> 0%
where the time goes in v1:
time: 230 us; the launch traced here: 229 us
  Pallas kernels  154 us (67%)
  local copies, waits for them, and re-layouts  40.6 us (18%)
  blocking collectives  32.3 us (14%)
    pallas_call x2, Pallas kernels, solve(): pl.pallas_call(functools.partial(solve_kernel, n_c, n_p), in_specs=[VMEM,...  132 us
    all_gather x1, blocking collectives, shards(): cam_all = lax.all_gather(camera, 'chain', axis=0, tiled=True)  32.3 us
    unnamed x81, local copies, waits for them, and re-layouts  29.5 us
    pallas_call x1, Pallas kernels, sweep_maps(): pl.pallas_call(maps_kernel, grid=(count,), in_specs=[ahead, ahead, back,...  15.7 us
    pallas_call x3, Pallas kernels, eliminate(): pl.pallas_call(functools.partial(eliminate_kernel, adjoint_out), in_specs...  6.09 us

profile of v1, /device:TPU:0, one launch (start us, length us, event | category | flops | bytes accessed | tf_op | source)
XLA Modules:
  0.0 229.4 jit_solution(8431840037540661271)
XLA Ops:
  0.7 0.8 copy.22
  1.5 0.8 fusion.refs_1_
  2.3 1.1 copy_bitcast_fusion
  3.4 1.4 reshape.67
  4.8 0.8 copy.16
  5.5 1.1 copy_bitcast_fusion.1
  6.6 0.6 fusion.1.refs_2_
  7.2 0.7 multiply_exponential_fusion
  7.9 0.6 slice_bitcast_fusion.1
  9.1 0.8 tile.14.damp_ref
  9.9 32.3 %all_gather.3.refs_0_ = f32[64,384]{1,0:T(8,128)S(1)} all-gather(f32[8,384]{1,0:T(8,128)S(1)} %copy-done.35), channel_id=1, replica_groups=mesh['chain'=8,'pts'=4] {'chain'}, dimensions={0}, use_global_device_ids=true | all-gather | bytes 110592 | tf_op jit(solution)/shard_map/all_gather | solution.py:467
  42.2 1.1 copy-done.5
  43.3 0.9 copy-done.15
  44.3 0.9 copy-done.18
  45.2 0.8 copy-done.25
  46.0 2.4 %eliminate.3 = f32[64,384]{1,0:T(8,128)S(1)} custom-call(f32[64,384]{1,0:T(8,128)S(1)} %all_gather.3.refs_0_, bf16[512,64]{1,0:T(8,128)(2,1)S(1)} %copy-done.18, bf16[64,512]{1,0:T(8,128)(2,1)S(1)} %copy-done.25, bf16[12,256,128]{2,1,0:T(8,128)(2,1)S(1)} %bitcast.31, bf16[6,256,128]{2,1,0:T(8,128)(2,1)S(1)} %bitcast.34, f32[2,256,128]{2,1,0:T(8,128)S(1)} %bitcast.37, ...), custom_call_target="tpu_custom_call" | custom-call | tf_op jit(solution)/shard_map/eliminate/pallas_call | solution.py:199
  48.4 0.6 copy-done.30
  49.1 1.6 reshape.69.dense_ref
  50.6 1.7 copy-done.2
  52.3 15.7 %sweep_maps.1 = (bf16[8,384,384]{2,1,0:T(8,128)(2,1)S(1)}, bf16[8,384,384]{2,1,0:T(8,128)(2,1)S(1)}, bf16[8,384,384]{2,1,0:T(8,128)(2,1)S(1)}, bf16[8,384,384]{2...) custom-call(bf16[8,384,384]{2,1,0:T(8,128)(2,1)S(1)} %copy-done.1, ...), custom_call_target="tpu_custom_call" | custom-call | tf_op jit(solution)/shard_map/sweep_maps/pallas_call | solution.py:79
  68.0 1.4 copy-done.14
  69.5 66.0 %solve.2 = (f32[8,384]{1,0:T(8,128)S(1)}, f32[8,8,384]{2,1,0:T(8,128)S(1)}) custom-call(f32[32,2,384]{2,1,0:T(2,128)S(1)} %copy-done.27, f32[8,384]{1,0:T(8,128)S(1)} %copy-done.35, f32[1,384]{1,0:T(1,128)S(1)} %tile.14.damp_ref, bf16[8,384,384]{2,1,0:T(8,128)(2,1)S(1)} %copy-done.1, bf16[8,384,384]{2,1,0:T(8,128)(2,1)S(1)} %copy-done.3, ...), custom_call_target="tpu_custom_call" | custom-call | tf_op jit(solution)/shard_map/solve/pallas_call | solution.py:423
  135.5 0.6 copy-done.33
  136.9 1.1 copy-done.6
  138.0 0.9 copy-done.16
  138.9 0.9 copy-done.19
  139.8 0.8 copy-done.26
  140.7 0.9 copy-done.34
  141.6 2.4 %eliminate.4 = f32[64,384]{1,0:T(8,128)S(1)} custom-call(f32[64,384]{1,0:T(8,128)S(1)} %bitcast.41, bf16[512,64]{1,0:T(8,128)(2,1)S(1)} %copy-done.19, bf16[64,512]{1,0:T(8,128)(2,1)S(1)} %copy-done.26, bf16[12,256,128]{2,1,0:T(8,128)(2,1)S(1)} %bitcast.32, bf16[6,256,128]{2,1,0:T(8,128)(2,1)S(1)} %bitcast.35, f32[2,256,128]{2,1,0:T(8,128)S(1)} %bitcast.38, ...), custom_call_target="tpu_custom_call" | custom-call | tf_op jit(solution)/shard_map/eliminate/pallas_call | solution.py:199
  144.0 0.6 copy-done.29
  144.6 1.6 reshape.71.dense_ref
  146.2 1.7 copy-done.4
  147.9 1.7 copy-done.9
  149.5 1.7 copy-done.11
  151.2 1.7 copy-done.13
  152.9 1.0 copy-done.22
  153.8 1.0 copy-done.24
  154.8 0.9 copy-done.28
  155.7 0.7 copy-done.37
  156.4 65.9 %solve.3 = (f32[8,384]{1,0:T(8,128)S(1)}, f32[8,8,384]{2,1,0:T(8,128)S(1)}) custom-call(f32[32,2,384]{2,1,0:T(2,128)S(1)} %copy-done.28, f32[8,384]{1,0:T(8,128)S(1)} %copy-done.37, f32[1,384]{1,0:T(1,128)S(1)} %tile.16.damp_ref, bf16[8,384,384]{2,1,0:T(8,128)(2,1)S(1)} %copy-done.1, bf16[8,384,384]{2,1,0:T(8,128)(2,1)S(1)} %copy-done.4, ...), custom_call_target="tpu_custom_call" | custom-call | tf_op jit(solution)/shard_map/solve/pallas_call | solution.py:423
  222.3 0.6 copy-done.31
  223.0 1.1 copy-done.7
  224.1 0.9 copy-done.17
  225.1 0.9 copy-done.20
  226.0 0.9 copy-done.32
  226.9 1.3 eliminate.5
  228.2 0.6 slice_bitcast_fusion
  228.8 0.6 copy.24
  (61 shorter events, 1.6 us)
Async XLA Ops:
  0.6 1.7 copy-start
  0.6 9.2 %copy-start.35 = (f32[8,384]{1,0:T(8,128)S(1)}, f32[8,384]{1,0:T(8,128)}, u32[]{:S(2)}) copy-start(f32[8,384]{1,0:T(8,128)} %cam_ref.1) | copy-start | bytes 36868
  3.4 47.3 %copy-start.1 = (bf16[8,384,384]{2,1,0:T(8,128)(2,1)S(1)}, bf16[8,384,384]{2,1,0:T(8,128)(2,1)}, u32[]{:S(2)}) copy-start(bf16[8,384,384]{2,1,0:T(8,128)(2,1)} %d_hbm.3) | copy-start | bytes 7077892
  42.2 1.1 copy-start.5
  43.3 0.9 copy-start.15
  44.3 0.9 copy-start.18
  45.2 0.8 copy-start.25
  48.4 0.6 copy-start.30
  50.6 1.7 copy-start.2
  52.3 17.1 %copy-start.3 = (bf16[8,384,384]{2,1,0:T(8,128)(2,1)S(1)}, bf16[8,384,384]{2,1,0:T(8,128)(2,1)}, u32[]{:S(2)}) copy-start(bf16[8,384,384]{2,1,0:T(8,128)(2,1)} %c_hbm.3) | copy-start | bytes 7077892
  52.3 17.2 %copy-start.27 = (f32[32,2,384]{2,1,0:T(2,128)S(1)}, f32[32,2,384]{2,1,0:T(2,128)}, u32[]{:S(2)}) copy-start(f32[32,2,384]{2,1,0:T(2,128)} %reshape.69.dense_ref) | copy-start | bytes 294916
  68.0 1.4 copy-start.14
  69.4 66.0 %copy-start.8 = (bf16[8,384,384]{2,1,0:T(8,128)(2,1)}, bf16[8,384,384]{2,1,0:T(8,128)(2,1)S(1)}, u32[]{:S(2)}) copy-start(bf16[8,384,384]{2,1,0:T(8,128)(2,1)S(1)} %get-tuple-element.12.wh_hbm) | copy-start | bytes 7077892
  69.4 66.0 %copy-start.10 = (bf16[8,384,384]{2,1,0:T(8,128)(2,1)}, bf16[8,384,384]{2,1,0:T(8,128)(2,1)S(1)}, u32[]{:S(2)}) copy-start(bf16[8,384,384]{2,1,0:T(8,128)(2,1)S(1)} %get-tuple-element.13.wl_hbm) | copy-start | bytes 7077892
  69.4 66.1 %copy-start.12 = (bf16[8,384,384]{2,1,0:T(8,128)(2,1)}, bf16[8,384,384]{2,1,0:T(8,128)(2,1)S(1)}, u32[]{:S(2)}) copy-start(bf16[8,384,384]{2,1,0:T(8,128)(2,1)S(1)} %get-tuple-element.14.xh_hbm) | copy-start | bytes 7077892
  69.4 66.1 %copy-start.21 = (bf16[384,384]{1,0:T(8,128)(2,1)}, bf16[384,384]{1,0:T(8,128)(2,1)S(1)}, u32[]{:S(2)}) copy-start(bf16[384,384]{1,0:T(8,128)(2,1)S(1)} %get-tuple-element.16.rh_ref) | copy-start | bytes 884740
  69.4 66.1 %copy-start.23 = (bf16[384,384]{1,0:T(8,128)(2,1)}, bf16[384,384]{1,0:T(8,128)(2,1)S(1)}, u32[]{:S(2)}) copy-start(bf16[384,384]{1,0:T(8,128)(2,1)S(1)} %get-tuple-element.17.rl_ref) | copy-start | bytes 884740
  69.5 67.3 %copy-start.38 = (f32[64]{0:T(128)S(1)}, f32[64]{0:T(128)}, u32[]{:S(2)}) copy-start(f32[64]{0:T(128)} %get-tuple-element.22) | copy-start | bytes 772
  135.5 0.6 copy-start.33
  136.2 0.6 copy-start.36
  136.9 1.1 copy-start.6
  138.0 0.9 copy-start.16
  138.9 0.9 copy-start.19
  139.8 0.8 copy-start.26
  140.7 0.9 copy-start.34
  144.0 0.6 copy-start.29
  146.2 1.7 copy-start.4
  147.9 1.7 copy-start.9
  149.5 1.7 copy-start.11
  151.2 1.7 copy-start.13
  152.9 1.0 copy-start.22
  153.8 1.0 copy-start.24
  154.8 0.9 copy-start.28
  155.7 0.7 copy-start.37
  156.4 66.5 %copy-start.39 = (f32[64]{0:T(128)S(1)}, f32[64]{0:T(128)}, u32[]{:S(2)}) copy-start(f32[64]{0:T(128)} %get-tuple-element.22) | copy-start | bytes 772
  222.2 0.6 copy-start.31
  223.0 1.1 copy-start.7
  224.1 0.9 copy-start.17
  225.1 0.9 copy-start.20
  226.0 0.9 copy-start.32

commit v2 on v1

v2 whole, which is shorter than its diff:
```python
import functools

import jax
import jax.numpy as jnp
from jax import lax
from jax.experimental import pallas as pl
from jax.experimental.pallas import tpu as pltpu
from jax.sharding import PartitionSpec as P

ITERS = 2
MESH = pl.DeviceIdType.MESH
F32, BF16 = jnp.float32, jnp.bfloat16
VMEM = pl.BlockSpec(memory_space=pltpu.VMEM)
ANY = pl.BlockSpec(memory_space=pl.ANY)


def dot_rows(x, panel):
    return lax.dot_general(x, panel, (((1,), (0,)), ((), ())), preferred_element_type=F32)


def dot_cols(x, panel):
    return lax.dot_general(x, panel, (((1,), (1,)), ((), ())), preferred_element_type=F32)


def halves(x):
    high = x.astype(BF16)
    return high, (x - high.astype(F32)).astype(BF16)


def thirds(x):
    high = x.astype(BF16)
    rest = x - high.astype(F32)
    mid = rest.astype(BF16)
    return high, mid, (rest - mid.astype(F32)).astype(BF16)


def eliminate(adjoint_out, cameras, pick_ref, pick_t_ref, cj_ref, pj_ref, res_ref, damp, out_ref, seen, parts):
    rows = res_ref.shape[1]
    blocks = rows // 4
    high, mid, low = thirds(cameras)
    pick = pick_ref[...]
    seen[...] = (dot_rows(pick, low) + dot_rows(pick, mid)) + dot_rows(pick, high)
    step = 16
    left = lax.broadcasted_iota(jnp.int32, (step, 128), 1) < 64

    def swap(x):
        return pltpu.roll(x, 64, 1)

    def chunk(i, carry):
        at = pl.multiple_of(i * step, step)
        misfits, points = [], []
        hess = [None] * 6
        target = [None] * 3
        pairs = ((0, 0), (0, 1), (0, 2), (1, 1), (1, 2), (2, 2))
        for tp in range(4):
            here = pl.ds(tp * blocks + at, step)
            there = pl.ds(rows + tp * blocks + at, step)
            cams = []
            for c in range(3):
                even = seen[here, c * 128 : (c + 1) * 128]
                odd = seen[there, c * 128 : (c + 1) * 128]
                cams.append(jnp.where(left, even, swap(odd)))
                cams.append(jnp.where(left, swap(even), odd))
            for a in range(2):
                miss = res_ref[a, here, :]
                for m in range(6):
                    miss = miss + cj_ref[6 * a + m, here, :].astype(F32) * cams[m]
                terms = [pj_ref[3 * a + n, here, :].astype(F32) for n in range(3)]
                misfits.append(miss)
                points.append(terms)
                for e, (n, k) in enumerate(pairs):
                    new = terms[n] * terms[k]
                    hess[e] = new if hess[e] is None else hess[e] + new
                for n in range(3):
                    new = terms[n] * miss
                    target[n] = new if target[n] is None else target[n] + new
        hess = [h + swap(h) for h in hess]
        ta, tb, tc = [t + swap(t) for t in target]
        aa, ab, ac, bb, bc, cc = hess
        aa, bb, cc = aa + damp, bb + damp, cc + damp
        cof_aa = bb * cc - bc * bc
        cof_ab = ac * bc - ab * cc
        cof_ac = ab * bc - ac * bb
        cof_bb = aa * cc - ac * ac
        cof_bc = ab * ac - aa * bc
        cof_cc = aa * bb - ab * ab
        det = aa * cof_aa + ab * cof_ab + ac * cof_ac
        sol = (
            (cof_aa * ta + cof_ab * tb + cof_ac * tc) / det,
            (cof_ab * ta + cof_bb * tb + cof_bc * tc) / det,
            (cof_ac * ta + cof_bc * tb + cof_cc * tc) / det,
        )
        if not adjoint_out:
            for n in range(3):
                out_ref[n, pl.ds(at, step), :] = -sol[n]
            return carry
        for tp in range(4):
            here = pl.ds(tp * blocks + at, step)
            there = pl.ds(rows + tp * blocks + at, step)
            left_over = []
            for a in range(2):
                terms = points[2 * tp + a]
                left_over.append(
                    misfits[2 * tp + a]
                    - (terms[0] * sol[0] + terms[1] * sol[1] + terms[2] * sol[2])
                )
            adj = [
                cj_ref[m, here, :].astype(F32) * left_over[0]
                + cj_ref[6 + m, here, :].astype(F32) * left_over[1]
                for m in range(6)
            ]
            for c in range(3):
                span = slice(c * 128, (c + 1) * 128)
                even = jnp.where(left, adj[2 * c], swap(adj[2 * c + 1]))
                odd = jnp.where(left, swap(adj[2 * c]), adj[2 * c + 1])
                for part, value in enumerate(thirds(even)):
                    parts[part, here, span] = value
                for part, value in enumerate(thirds(odd)):
                    parts[part, there, span] = value
        return carry

    lax.fori_loop(0, blocks // step, chunk, 0)
    if adjoint_out:
        pick_t = pick_t_ref[...]
        out_ref[...] = (
            dot_rows(pick_t, parts[2]) + dot_rows(pick_t, parts[1])
        ) + dot_rows(pick_t, parts[0])


def split_row(v):
    row = lax.broadcasted_iota(jnp.int32, v.shape, 0)
    high = v.astype(BF16).astype(F32)
    rest = v - high
    mid = rest.astype(BF16).astype(F32)
    low = rest - mid
    return jnp.where(row == 0, high, jnp.where(row == 1, mid, jnp.where(row == 2, low, 0.0))).astype(BF16)


def total(y):
    return jnp.broadcast_to(jnp.sum(y, axis=0, keepdims=True), y.shape)


def times(v, panel):
    return total(dot_rows(split_row(v), panel))


def times_t(v, panel):
    return total(dot_cols(split_row(v), panel))


def stacked(dot, x, panel):
    rows = x.shape[0]
    both = dot(jnp.concatenate(halves(x), axis=0), panel)
    return both[:rows] + both[rows:]


def whole_kernel(
    n_c, n_p,
    order_ref, cam_ref, damp_ref, cj_hbm, pj_hbm, res_hbm, d_hbm, c_hbm,
    cam_out, point_out,
    cj_ref, pj_ref, res_ref, d_ref, c_ref, wh_ref, wl_ref, xh_ref, xl_ref, rh_ref, rl_ref, run_f, run_b,
    pick, pick_t, seen, parts, dense, own, every,
    landed, piece, grad, solved, update, carry_in, carry_out,
    load_sem, rs_send, rs_recv, pts_send, pts_recv, ring_send, ring_recv, all_send, all_recv,
):
    me_c, me_p = lax.axis_index("chain"), lax.axis_index("pts")
    count, width = cam_ref.shape
    rows = res_ref.shape[1]
    loads = [
        pltpu.make_async_copy(src, dst, load_sem.at[i])
        for i, (src, dst) in enumerate(
            ((d_hbm, d_ref), (c_hbm, c_ref), (cj_hbm, cj_ref), (pj_hbm, pj_ref), (res_hbm, res_ref))
        )
    ]
    for load in loads:
        load.start()

    barrier = pltpu.get_barrier_semaphore()

    @pl.loop(1, n_c)
    def _(i):
        pl.semaphore_signal(
            barrier, inc=1, device_id=(lax.rem(me_c + i, n_c), me_p), device_id_type=MESH
        )

    for i in range(1, n_p):
        pl.semaphore_signal(
            barrier, inc=1, device_id=(me_c, lax.rem(me_p + i, n_p)), device_id_type=MESH
        )
    pl.semaphore_wait(barrier, n_c + n_p - 2)

    def all_copy(turn, i):
        return pltpu.make_async_remote_copy(
            src_ref=own.at[turn],
            dst_ref=every.at[turn, me_c],
            send_sem=all_send.at[turn, i],
            recv_sem=all_recv.at[turn, i],
            device_id=(lax.rem(me_c + i, n_c), me_p),
            device_id_type=MESH,
        )

    def share_camera(turn):
        @pl.loop(1, n_c)
        def _(i):
            all_copy(turn, i).start()

        every[turn, me_c] = own[turn]

    def await_cameras(turn):
        @pl.loop(1, n_c)
        def _(i):
            all_copy(turn, i).wait()

    own[0] = cam_ref[...]
    share_camera(0)

    cams = lax.broadcasted_iota(jnp.int32, pick_t.shape, 0)
    chosen = jnp.where(cams == jnp.broadcast_to(order_ref[...], pick_t.shape), 1.0, 0.0)
    pick_t[...] = chosen.astype(BF16)
    pick[...] = chosen.T.astype(BF16)

    unit = (
        lax.broadcasted_iota(jnp.int32, (width, width), 0)
        == lax.broadcasted_iota(jnp.int32, (width, width), 1)
    ).astype(F32)
    run_f[...] = unit
    run_b[...] = unit

    def map_step(k, carry):
        back = count - 1 - k
        made = -stacked(dot_rows, run_f[...], d_ref[k])
        high, low = halves(made)
        wh_ref[k] = high
        wl_ref[k] = low
        run_f[...] = stacked(dot_rows, made, c_ref[k])
        made = stacked(dot_cols, -stacked(dot_cols, run_b[...], c_ref[back]), d_ref[back])
        run_b[...] = made
        high, low = halves(made)
        xh_ref[back] = high
        xl_ref[back] = low
        return carry

    loads[0].wait()
    loads[1].wait()
    lax.fori_loop(0, 2, map_step, 0)
    for load in loads[2:]:
        load.wait()
    await_cameras(0)

    def zero_ahead():
        carried = None
        for k in range(count):
            g = jnp.broadcast_to(grad[k : k + 1, :], carry_in.shape[2:])
            s = times(g if carried is None else g - carried, d_ref[k])
            solved[k : k + 1, :] = s[0:1]
            if k < count - 1:
                carried = times(s, c_ref[k])

    def zero_back():
        later = None
        for k in reversed(range(count)):
            r = jnp.broadcast_to(solved[k : k + 1, :], carry_in.shape[2:])
            if later is not None:
                r = r - times_t(later, c_ref[k])
            later = times_t(r, d_ref[k])
            update[k : k + 1, :] = later[0:1]

    def reach(vectors, high_ref, low_ref):
        acc = None
        for k in range(count):
            x = split_row(jnp.broadcast_to(vectors[k : k + 1, :], carry_in.shape[2:]))
            new = dot_cols(x, high_ref[k]) + dot_cols(x, low_ref[k])
            acc = new if acc is None else acc + new
        return -total(acc)

    def correct(x, out, high_ref, low_ref):
        for k in range(count):
            y = dot_rows(x, high_ref[k]) + dot_rows(x, low_ref[k])
            out[k : k + 1, :] = out[k : k + 1, :] + jnp.sum(y, axis=0, keepdims=True)

    def inner_step(it, carry):
        damp = damp_ref[it]
        cameras = every[it].reshape(n_c * count, width)
        eliminate(True, cameras, pick, pick_t, cj_ref, pj_ref, res_ref, damp[:, :128], dense, seen, parts)

        def rs_copy(i):
            to = lax.rem(me_c + i, n_c)
            return pltpu.make_async_remote_copy(
                src_ref=dense.at[pl.ds(pl.multiple_of(to * count, count), count)],
                dst_ref=landed.at[it, i],
                send_sem=rs_send.at[it, i],
                recv_sem=rs_recv.at[it, i],
                device_id=(to, me_p),
                device_id_type=MESH,
            )

        @pl.loop(1, n_c)
        def _(i):
            rs_copy(i).start()

        landed[it, 0] = dense[pl.ds(pl.multiple_of(me_c * count, count), count), :]

        @pl.when(it == 0)
        def _():
            lax.fori_loop(2, count, map_step, 0)
            high, low = halves(run_f[...])
            rh_ref[...] = high
            rl_ref[...] = low

        @pl.loop(1, n_c)
        def _(i):
            rs_copy(i).wait()

        mine = jnp.sum(landed[it], axis=0)

        def pts_copy(i):
            return pltpu.make_async_remote_copy(
                src_ref=piece.at[it, me_p],
                dst_ref=piece.at[it, me_p],
                send_sem=pts_send.at[it, i],
                recv_sem=pts_recv.at[it, i],
                device_id=(me_c, lax.rem(me_p + i, n_p)),
                device_id_type=MESH,
            )

        piece[it, me_p] = mine
        for i in range(1, n_p):
            pts_copy(i).start()
        for i in range(1, n_p):
            pts_copy(i).wait()
        grad[...] = jnp.sum(piece[it], axis=0) + damp * own[it]

        def ring(way):
            to = lax.rem(me_c + (n_c - 1 if way else 1), n_c)
            return pltpu.make_async_remote_copy(
                src_ref=carry_out.at[it, way], dst_ref=carry_in.at[it, way],
                send_sem=ring_send.at[it, way], recv_sem=ring_recv.at[it, way],
                device_id=(to, me_p), device_id_type=MESH,
            )

        def pass_on(way, reached, map_high, map_low, sweep):
            turn = n_c - 1 - me_c if way else me_c

            @pl.when(turn >= 3)
            def _():
                sweep()

            @pl.when(turn == 0)
            def _():
                carry_in[it, way] = jnp.zeros(carry_in.shape[2:], F32)

            @pl.when(turn > 0)
            def _():
                ring(way).wait_recv()

            x = split_row(carry_in[it, way])
            carry_out[it, way] = reached + total(dot_rows(x, map_high) + dot_rows(x, map_low))

            @pl.when(turn < n_c - 1)
            def _():
                ring(way).start()

            @pl.when(turn < 3)
            def _():
                sweep()

            return x

        x = pass_on(0, reach(grad, xh_ref, xl_ref), rh_ref[...], rl_ref[...], zero_ahead)
        correct(x, solved, wh_ref, wl_ref)
        x = pass_on(1, reach(solved, wh_ref, wl_ref), xh_ref[0], xl_ref[0], zero_back)
        correct(x, update, xh_ref, xl_ref)
        own[it + 1] = own[it] - update[...]
        share_camera(it + 1)

        @pl.when(me_c < n_c - 1)
        def _():
            ring(0).wait_send()

        @pl.when(me_c > 0)
        def _():
            ring(1).wait_send()

        await_cameras(it + 1)
        return carry

    lax.fori_loop(0, ITERS, inner_step, 0)
    cam_out[...] = own[ITERS]
    cameras = every[ITERS].reshape(n_c * count, width)
    eliminate(
        False, cameras, pick, pick_t, cj_ref, pj_ref, res_ref, damp_ref[ITERS - 1][:, :128], point_out, seen, parts
    )


def shards(n_c, n_p, cam_jac, point_jac, residual, obs_cam, damp_exp, cam_step, diag_inverse, coupling):
    blocks, observers = obs_cam.shape
    count, width = cam_step.shape
    total_blocks = count * n_c
    pairs = observers // 2
    rows = pairs * blocks

    def by_pair(x):
        comps = x.shape[1]
        return x.reshape(blocks, comps, pairs, 128).transpose(1, 2, 0, 3).reshape(comps, rows, 128)

    cj, pj, res = by_pair(cam_jac), by_pair(point_jac), by_pair(residual)
    order = obs_cam.reshape(blocks, pairs, 2).transpose(2, 1, 0).reshape(1, -1)
    wide = jnp.tile(jnp.exp2(damp_exp.astype(F32)), (1, 6))[:, None, :]
    panel = pltpu.VMEM((count, width, width), BF16)
    square = (width, width)
    sem = pltpu.SemaphoreType.DMA
    camera, out = pl.pallas_call(
        functools.partial(whole_kernel, n_c, n_p),
        in_specs=[VMEM] * 3 + [ANY] * 5,
        out_specs=[VMEM, VMEM],
        out_shape=[
            jax.ShapeDtypeStruct((count, width), F32),
            jax.ShapeDtypeStruct((3, blocks, 128), F32),
        ],
        scratch_shapes=[pltpu.VMEM(x.shape, x.dtype) for x in (cj, pj, res)]
        + [panel] * 6
        + [pltpu.VMEM(square, BF16)] * 2
        + [pltpu.VMEM(square, F32)] * 2
        + [
            pltpu.VMEM((2 * rows, total_blocks), BF16),
            pltpu.VMEM((total_blocks, 2 * rows), BF16),
            pltpu.VMEM((2 * rows, width), F32),
            pltpu.VMEM((3, 2 * rows, width), BF16),
            pltpu.VMEM((total_blocks, width), F32),
            pltpu.VMEM((ITERS + 1, count, width), F32),
            pltpu.VMEM((ITERS + 1, n_c, count, width), F32),
            pltpu.VMEM((ITERS, n_c, count, width), F32),
            pltpu.VMEM((ITERS, n_p, count, width), F32),
            pltpu.VMEM((count, width), F32),
            pltpu.VMEM((count, width), F32),
            pltpu.VMEM((count, width), F32),
            pltpu.VMEM((ITERS, 2, 8, width), F32),
            pltpu.VMEM((ITERS, 2, 8, width), F32),
            sem((5,)), sem((ITERS, n_c)), sem((ITERS, n_c)), sem((ITERS, n_p)), sem((ITERS, n_p)),
            sem((ITERS, 2)), sem((ITERS, 2)), sem((ITERS + 1, n_c)), sem((ITERS + 1, n_c)),
        ],
        compiler_params=pltpu.CompilerParams(
            collective_id=0, has_side_effects=True, vmem_limit_bytes=48 << 20
        ),
        name="camera_steps",
    )(order, cam_step, wide, cj, pj, res, diag_inverse, coupling)
    return camera, out[:, :, :64].transpose(1, 0, 2)


def solution(mesh):
    in_specs = (
        P(("chain", "pts"), None, None),
        P(("chain", "pts"), None, None),
        P(("chain", "pts"), None, None),
        P(("chain", "pts"), None),
        P(),
        P("chain", None),
        P("chain", None, None),
        P("chain", None, None),
    )
    out_specs = (P("chain", None), P(("chain", "pts"), None, None))
    inner = functools.partial(shards, mesh.shape["chain"], mesh.shape["pts"])
    return jax.shard_map(inner, mesh=mesh, in_specs=in_specs, out_specs=out_specs, check_vma=False)
```

time: 230 us -> 147 us (0.64)
  local copies, waits for them, and re-layouts: 40.6 us -> 4.77 us
  blocking collectives: 32.3 us -> 0 us
  Pallas kernels: 154 us -> 141 us
    all_gather x1 -> x0, blocking collectives: 32.3 us -> none  [shards(): cam_all = lax.all_gather(camera, 'chain', axis=0, tiled=True)]
    unnamed x81 -> x7, local copies, waits for them, and re-layouts: 29.5 us -> 0.62 us
    pallas_call x6 -> x1, Pallas kernels: 154 us -> 141 us  [shards(): pl.pallas_call(functools.partial(whole_kernel, n_c, n_p), in_specs=[VMEM]...]
    reshape x3 -> x2, local copies, waits for them, and re-layouts: 3.92 us -> 0.88 us  [shards(): order = obs_cam.reshape(blocks, pairs, 2).transpose(2, 1, 0).reshape(1, -1)]
where the time goes in v2:
time: 147 us
  Pallas kernels  141 us (96%)
  local copies, waits for them, and re-layouts  4.77 us (3%)
    pallas_call x1, Pallas kernels, shards(): pl.pallas_call(functools.partial(whole_kernel, n_c, n_p), in_specs=[VMEM]...  141 us

profile of v2, /device:TPU:0, one launch (start us, length us, event | category | flops | bytes accessed | tf_op | source)
XLA Modules:
  0.0 147.2 jit_solution(7330817897757072288)
XLA Ops:
  0.6 0.0 copy-start
  0.6 0.0 copy-start.1
  0.7 0.0 copy-start.2
  0.7 0.8 multiply_exponential_fusion
  1.5 0.8 copy.24
  2.3 0.1 reshape.35.order_ref
  2.4 0.1 tile.10.damp_ref
  2.5 1.2 reshape.40
  3.7 0.1 copy.17
  3.7 1.1 copy_bitcast_fusion.1
  4.8 0.0 copy-done
  4.8 0.2 copy_bitcast_fusion
  5.0 0.0 copy-done.1
  5.1 0.0 copy-done.2
  5.1 140.9 %camera_steps.1 = (f32[8,384]{1,0:T(8,128)S(1)}, f32[3,64,128]{2,1,0:T(8,128)S(1)}) custom-call(s32[1,512]{1,0:T(1,128)S(1)} %reshape.35.order_ref, f32[8,384]{1,0:T(8,128)S(1)} %copy-done.2, f32[2,1,384]{2,1,0:T(1,128)S(1)} %tile.10.damp_ref, bf16[12,256,128]{2,1,0:T(8,128)(2,1)S(1)} %bitcast.25, bf16[6,256,128]{2,1,0:T(8,128)(2,1)S(1)} %bitcast.26, ...), custom_call_target="tpu_custom_call" | custom-call | tf_op jit(solution)/shard_map/camera_steps/pallas_call | solution.py:412
  146.0 0.6 slice_bitcast_fusion
  146.6 0.6 copy.26
  (1 shorter events, 0.0 us)
Async XLA Ops:
  0.6 4.2 %copy-start = (bf16[64,12,512]{2,0,1:T(8,128)(2,1)S(1)}, bf16[64,12,512]{2,0,1:T(8,128)(2,1)}, u32[]{:S(2)}) copy-start(bf16[64,12,512]{2,0,1:T(8,128)(2,1)} %param.8) | copy-start | bytes 2359300
  0.6 4.4 %copy-start.1 = (bf16[8,384,384]{2,1,0:T(8,128)(2,1)S(1)}, bf16[8,384,384]{2,1,0:T(8,128)(2,1)}, u32[]{:S(2)}) copy-start(bf16[8,384,384]{2,1,0:T(8,128)(2,1)} %d_hbm.1) | copy-start | bytes 7077892
  0.7 4.4 %copy-start.2 = (f32[8,384]{1,0:T(8,128)S(1)}, f32[8,384]{1,0:T(8,128)}, u32[]{:S(2)}) copy-start(f32[8,384]{1,0:T(8,128)} %cam_ref.1) | copy-start | bytes 36868

commit v3 on v2

--- a/solution.py
+++ b/solution.py
@@ -160,8 +160,9 @@
     cam_out, point_out,
     cj_ref, pj_ref, res_ref, d_ref, c_ref, wh_ref, wl_ref, xh_ref, xl_ref, rh_ref, rl_ref, run_f, run_b,
     pick, pick_t, seen, parts, dense, own, every,
-    landed, piece, grad, solved, update, carry_in, carry_out,
-    load_sem, rs_send, rs_recv, pts_send, pts_recv, ring_send, ring_recv, all_send, all_recv,
+    landed, piece, grad, solved, update, carry_in, carry_out, first_in, first_out, entry,
+    run_nb, nh_ref, nl_ref, ph_ref, pk_ref,
+    load_sem, rs_send, rs_recv, pts_send, pts_recv, ring_send, ring_recv, first_send, first_recv, all_send, all_recv, nb_send, nb_recv,
 ):
     me_c, me_p = lax.axis_index("chain"), lax.axis_index("pts")
     count, width = cam_ref.shape
@@ -226,23 +227,45 @@
     run_f[...] = unit
     run_b[...] = unit
 
-    def map_step(k, carry):
-        back = count - 1 - k
+    def map_ahead(k, carry):
         made = -stacked(dot_rows, run_f[...], d_ref[k])
         high, low = halves(made)
         wh_ref[k] = high
         wl_ref[k] = low
         run_f[...] = stacked(dot_rows, made, c_ref[k])
-        made = stacked(dot_cols, -stacked(dot_cols, run_b[...], c_ref[back]), d_ref[back])
+        return carry
+
+    def map_back(i, carry):
+        k = count - 1 - i
+        made = stacked(dot_cols, -stacked(dot_cols, run_b[...], c_ref[k]), d_ref[k])
         run_b[...] = made
         high, low = halves(made)
-        xh_ref[back] = high
-        xl_ref[back] = low
+        xh_ref[k] = high
+        xl_ref[k] = low
         return carry
+
+    odd = lax.rem(me_c, 2)
+    swap_maps = pltpu.make_async_remote_copy(
+        src_ref=run_f, dst_ref=run_nb, send_sem=nb_send, recv_sem=nb_recv,
+        device_id=(me_c + 1 - 2 * odd, me_p), device_id_type=MESH,
+    )
+
+    def pair_map():
+        high, low = halves(run_f[...])
+        rh_ref[...] = high
+        rl_ref[...] = low
+        swap_maps.wait()
+        mine, other = run_f[...], run_nb[...]
+        nh_ref[...], nl_ref[...] = halves(other)
+        early = jnp.where(odd == 1, other, mine)
+        late_high, late_low = halves(jnp.where(odd == 1, mine, other))
+        high, low = halves(stacked(dot_rows, early, late_high) + stacked(dot_rows, early, late_low))
+        ph_ref[...] = high
+        pk_ref[...] = low
 
     loads[0].wait()
     loads[1].wait()
-    lax.fori_loop(0, 2, map_step, 0)
+    lax.fori_loop(0, 4, map_ahead, 0)
     for load in loads[2:]:
         load.wait()
     await_cameras(0)
@@ -302,10 +325,10 @@
 
         @pl.when(it == 0)
         def _():
-            lax.fori_loop(2, count, map_step, 0)
-            high, low = halves(run_f[...])
-            rh_ref[...] = high
-            rl_ref[...] = low
+            lax.fori_loop(4, count, map_ahead, 0)
+            swap_maps.start()
+            lax.fori_loop(0, count, map_back, 0)
+            pair_map()
 
         @pl.loop(1, n_c)
         def _(i):
@@ -330,57 +353,95 @@
             pts_copy(i).wait()
         grad[...] = jnp.sum(piece[it], axis=0) + damp * own[it]
 
-        def ring(way):
-            to = lax.rem(me_c + (n_c - 1 if way else 1), n_c)
+        def hand(way):
+            return pltpu.make_async_remote_copy(
+                src_ref=first_out.at[it, way], dst_ref=first_in.at[it, way],
+                send_sem=first_send.at[it, way], recv_sem=first_recv.at[it, way],
+                device_id=(me_c + 1 - 2 * odd, me_p), device_id_type=MESH,
+            )
+
+        def ring(way, far):
+            to = lax.rem(me_c + (n_c - far if way else far), n_c)
             return pltpu.make_async_remote_copy(
                 src_ref=carry_out.at[it, way], dst_ref=carry_in.at[it, way],
-                send_sem=ring_send.at[it, way], recv_sem=ring_recv.at[it, way],
+                send_sem=ring_send.at[it, way, far - 1], recv_sem=ring_recv.at[it, way],
                 device_id=(to, me_p), device_id_type=MESH,
             )
 
+        def seat(way):
+            turn = n_c - 1 - me_c if way else me_c
+            return lax.rem(turn, 2) == 1, turn // 2
+
         def pass_on(way, reached, map_high, map_low, sweep):
-            turn = n_c - 1 - me_c if way else me_c
-
-            @pl.when(turn >= 3)
+            second, group = seat(way)
+            dot = dot_cols if way else dot_rows
+
+            def arrive():
+                @pl.when(group == 0)
+                def _():
+                    carry_in[it, way] = jnp.zeros(carry_in.shape[2:], F32)
+
+                @pl.when(group > 0)
+                def _():
+                    ring(way, 2).wait_recv()
+
+                return carry_in[it, way]
+
+            first_out[it, way] = reached
+
+            @pl.when(jnp.logical_not(second))
             def _():
+                hand(way).start()
                 sweep()
-
-            @pl.when(turn == 0)
+                entry[...] = arrive()
+
+            @pl.when(second)
             def _():
-                carry_in[it, way] = jnp.zeros(carry_in.shape[2:], F32)
-
-            @pl.when(turn > 0)
+                @pl.when(group >= 2)
+                def _():
+                    sweep()
+
+                hand(way).wait_recv()
+                given = first_in[it, way]
+                x = split_row(given)
+                both = first_out[it, way] + total(dot_rows(x, map_high[...]) + dot_rows(x, map_low[...]))
+                x = split_row(arrive())
+                carry_out[it, way] = both + total(dot(x, ph_ref[...]) + dot(x, pk_ref[...]))
+
+                @pl.when(group < n_c // 2 - 1)
+                def _():
+                    ring(way, 2).start()
+                    ring(way, 1).start()
+
+                entry[...] = given + total(dot(x, nh_ref[...]) + dot(x, nl_ref[...]))
+
+                @pl.when(group < 2)
+                def _():
+                    sweep()
+
+            return split_row(entry[...])
+
+        def drain(way):
+            second, group = seat(way)
+
+            @pl.when(jnp.logical_not(second))
             def _():
-                ring(way).wait_recv()
-
-            x = split_row(carry_in[it, way])
-            carry_out[it, way] = reached + total(dot_rows(x, map_high) + dot_rows(x, map_low))
-
-            @pl.when(turn < n_c - 1)
+                hand(way).wait_send()
+
+            @pl.when(jnp.logical_and(second, group < n_c // 2 - 1))
             def _():
-                ring(way).start()
-
-            @pl.when(turn < 3)
-            def _():
-                sweep()
-
-            return x
-
-        x = pass_on(0, reach(grad, xh_ref, xl_ref), rh_ref[...], rl_ref[...], zero_ahead)
+                ring(way, 2).wait_send()
+                ring(way, 1).wait_send()
+
+        x = pass_on(0, reach(grad, xh_ref, xl_ref), rh_ref, rl_ref, zero_ahead)
         correct(x, solved, wh_ref, wl_ref)
-        x = pass_on(1, reach(solved, wh_ref, wl_ref), xh_ref[0], xl_ref[0], zero_back)
+        x = pass_on(1, reach(solved, wh_ref, wl_ref), xh_ref.at[0], xl_ref.at[0], zero_back)
         correct(x, update, xh_ref, xl_ref)
         own[it + 1] = own[it] - update[...]
         share_camera(it + 1)
 
-        @pl.when(me_c < n_c - 1)
-        def _():
-            ring(0).wait_send()
-
-        @pl.when(me_c > 0)
-        def _():
-            ring(1).wait_send()
-
+        drain(0)
+        drain(1)
         await_cameras(it + 1)
         return carry
 
@@ -436,8 +497,17 @@
             pltpu.VMEM((count, width), F32),
             pltpu.VMEM((ITERS, 2, 8, width), F32),
             pltpu.VMEM((ITERS, 2, 8, width), F32),
+            pltpu.VMEM((ITERS, 2, 8, width), F32),
+            pltpu.VMEM((ITERS, 2, 8, width), F32),
+            pltpu.VMEM((8, width), F32),
+            pltpu.VMEM(square, F32),
+            pltpu.VMEM(square, BF16),
+            pltpu.VMEM(square, BF16),
+            pltpu.VMEM(square, BF16),
+            pltpu.VMEM(square, BF16),
             sem((5,)), sem((ITERS, n_c)), sem((ITERS, n_c)), sem((ITERS, n_p)), sem((ITERS, n_p)),
-            sem((ITERS, 2)), sem((ITERS, 2)), sem((ITERS + 1, n_c)), sem((ITERS + 1, n_c)),
+            sem((ITERS, 2, 2)), sem((ITERS, 2)), sem((ITERS, 2)), sem((ITERS, 2)),
+            sem((ITERS + 1, n_c)), sem((ITERS + 1, n_c)), sem(()), sem(()),
         ],
         compiler_params=pltpu.CompilerParams(
             collective_id=0, has_side_effects=True, vmem_limit_bytes=48 << 20

time: 147 us -> 118 us (0.80)
  Pallas kernels: 141 us -> 112 us
    pallas_call x1, Pallas kernels: 141 us -> 112 us  [shards(): pl.pallas_call(functools.partial(whole_kernel, n_c, n_p), in_specs=[VMEM]...]
where the time goes in v3:
time: 118 us
  Pallas kernels  112 us (95%)
  local copies, waits for them, and re-layouts  4.77 us (4%)
    pallas_call x1, Pallas kernels, shards(): pl.pallas_call(functools.partial(whole_kernel, n_c, n_p), in_specs=[VMEM]...  112 us
    reshape x4, local copies, waits for them, and re-layouts, by_pair(): x.reshape(blocks, comps, pairs, 128).transpose(1, 2, 0, 3)  2.54 us

profile of v3, /device:TPU:0, one launch (start us, length us, event | category | flops | bytes accessed | tf_op | source)
XLA Modules:
  0.0 118.1 jit_solution(290273431095181625)
XLA Ops:
  0.6 0.0 copy-start
  0.6 0.0 copy-start.1
  0.7 0.0 copy-start.2
  0.7 0.8 multiply_exponential_fusion
  1.5 0.8 copy.24
  2.3 0.1 reshape.35.order_ref
  2.4 0.1 tile.10.damp_ref
  2.5 1.2 %reshape.40 = f32[64,2,4,128]{3,2,1,0:T(4,128)S(1)} reshape(f32[64,2,512]{2,1,0:T(2,128)} %param.10) | data formatting | bytes 524288 | tf_op jit(solution)/shard_map/reshape | solution.py:465
  3.7 0.1 copy.17
  3.7 1.1 copy_bitcast_fusion.1
  4.8 0.0 copy-done
  4.8 0.2 copy_bitcast_fusion
  5.0 0.0 copy-done.1
  5.1 0.0 copy-done.2
  5.1 111.8 %camera_steps.1 = (f32[8,384]{1,0:T(8,128)S(1)}, f32[3,64,128]{2,1,0:T(8,128)S(1)}) custom-call(s32[1,512]{1,0:T(1,128)S(1)} %reshape.35.order_ref, f32[8,384]{1,0:T(8,128)S(1)} %copy-done.2, f32[2,1,384]{2,1,0:T(1,128)S(1)} %tile.10.damp_ref, bf16[12,256,128]{2,1,0:T(8,128)(2,1)S(1)} %bitcast.25, bf16[6,256,128]{2,1,0:T(8,128)(2,1)S(1)} %bitcast.26, ...), custom_call_target="tpu_custom_call" | custom-call | tf_op jit(solution)/shard_map/camera_steps/pallas_call | solution.py:473
  116.9 0.6 slice_bitcast_fusion
  117.5 0.6 copy.26
  (1 shorter events, 0.0 us)
Async XLA Ops:
  0.6 4.2 %copy-start = (bf16[64,12,512]{2,0,1:T(8,128)(2,1)S(1)}, bf16[64,12,512]{2,0,1:T(8,128)(2,1)}, u32[]{:S(2)}) copy-start(bf16[64,12,512]{2,0,1:T(8,128)(2,1)} %param.8) | copy-start | bytes 2359300
  0.6 4.4 %copy-start.1 = (bf16[8,384,384]{2,1,0:T(8,128)(2,1)S(1)}, bf16[8,384,384]{2,1,0:T(8,128)(2,1)}, u32[]{:S(2)}) copy-start(bf16[8,384,384]{2,1,0:T(8,128)(2,1)} %d_hbm.1) | copy-start | bytes 7077892
  0.7 4.4 %copy-start.2 = (f32[8,384]{1,0:T(8,128)S(1)}, f32[8,384]{1,0:T(8,128)}, u32[]{:S(2)}) copy-start(f32[8,384]{1,0:T(8,128)} %cam_ref.1) | copy-start | bytes 36868

commit v4 on v3

--- a/solution.py
+++ b/solution.py
@@ -265,7 +265,8 @@
 
     loads[0].wait()
     loads[1].wait()
-    lax.fori_loop(0, 4, map_ahead, 0)
+    lax.fori_loop(0, count, map_ahead, 0)
+    swap_maps.start()
     for load in loads[2:]:
         load.wait()
     await_cameras(0)
@@ -325,10 +326,7 @@
 
         @pl.when(it == 0)
         def _():
-            lax.fori_loop(4, count, map_ahead, 0)
-            swap_maps.start()
             lax.fori_loop(0, count, map_back, 0)
-            pair_map()
 
         @pl.loop(1, n_c)
         def _(i):
@@ -349,6 +347,11 @@
         piece[it, me_p] = mine
         for i in range(1, n_p):
             pts_copy(i).start()
+
+        @pl.when(it == 0)
+        def _():
+            pair_map()
+
         for i in range(1, n_p):
             pts_copy(i).wait()
         grad[...] = jnp.sum(piece[it], axis=0) + damp * own[it]

time: 118 us -> 116 us (0.983)
  Pallas kernels: 112 us -> 109 us
    pallas_call x1, Pallas kernels: 112 us -> 109 us  [shards(): pl.pallas_call(functools.partial(whole_kernel, n_c, n_p), in_specs=[VMEM]...]
where the time goes in v4:
time: 116 us
  Pallas kernels  109 us (94%)
  local copies, waits for them, and re-layouts  4.77 us (4%)
    pallas_call x1, Pallas kernels, shards(): pl.pallas_call(functools.partial(whole_kernel, n_c, n_p), in_specs=[VMEM]...  109 us
    reshape x4, local copies, waits for them, and re-layouts, by_pair(): x.reshape(blocks, comps, pairs, 128).transpose(1, 2, 0, 3)  2.54 us

profile of v4, /device:TPU:0, one launch (start us, length us, event | category | flops | bytes accessed | tf_op | source)
XLA Modules:
  0.0 115.6 jit_solution(11623829286243513583)
XLA Ops:
  0.6 0.0 copy-start
  0.6 0.0 copy-start.1
  0.7 0.0 copy-start.2
  0.7 0.8 multiply_exponential_fusion
  1.5 0.8 copy.24
  2.3 0.1 reshape.35.order_ref
  2.4 0.1 tile.10.damp_ref
  2.5 1.2 %reshape.40 = f32[64,2,4,128]{3,2,1,0:T(4,128)S(1)} reshape(f32[64,2,512]{2,1,0:T(2,128)} %param.10) | data formatting | bytes 524288 | tf_op jit(solution)/shard_map/reshape | solution.py:468
  3.7 0.1 copy.17
  3.7 1.1 copy_bitcast_fusion.1
  4.8 0.0 copy-done
  4.8 0.2 copy_bitcast_fusion
  5.0 0.0 copy-done.1
  5.1 0.0 copy-done.2
  5.1 109.3 %camera_steps.1 = (f32[8,384]{1,0:T(8,128)S(1)}, f32[3,64,128]{2,1,0:T(8,128)S(1)}) custom-call(s32[1,512]{1,0:T(1,128)S(1)} %reshape.35.order_ref, f32[8,384]{1,0:T(8,128)S(1)} %copy-done.2, f32[2,1,384]{2,1,0:T(1,128)S(1)} %tile.10.damp_ref, bf16[12,256,128]{2,1,0:T(8,128)(2,1)S(1)} %bitcast.25, bf16[6,256,128]{2,1,0:T(8,128)(2,1)S(1)} %bitcast.26, ...), custom_call_target="tpu_custom_call" | custom-call | tf_op jit(solution)/shard_map/camera_steps/pallas_call | solution.py:476
  114.3 0.6 slice_bitcast_fusion
  115.0 0.6 copy.26
  (1 shorter events, 0.0 us)
Async XLA Ops:
  0.6 4.2 %copy-start = (bf16[64,12,512]{2,0,1:T(8,128)(2,1)S(1)}, bf16[64,12,512]{2,0,1:T(8,128)(2,1)}, u32[]{:S(2)}) copy-start(bf16[64,12,512]{2,0,1:T(8,128)(2,1)} %param.8) | copy-start | bytes 2359300
  0.6 4.4 %copy-start.1 = (bf16[8,384,384]{2,1,0:T(8,128)(2,1)S(1)}, bf16[8,384,384]{2,1,0:T(8,128)(2,1)}, u32[]{:S(2)}) copy-start(bf16[8,384,384]{2,1,0:T(8,128)(2,1)} %d_hbm.1) | copy-start | bytes 7077892
  0.7 4.4 %copy-start.2 = (f32[8,384]{1,0:T(8,128)S(1)}, f32[8,384]{1,0:T(8,128)}, u32[]{:S(2)}) copy-start(f32[8,384]{1,0:T(8,128)} %cam_ref.1) | copy-start | bytes 36868
